TPU v7x, 512 devices: a whole 4x8x8 slice. The times are simulated.
512 devices in a mesh: seq: 64 (over y, x, core), dp: 8 (over z).
Axes of the slice: x: 4, y: 8, z: 8, core: 2. Of those that a mesh axis runs over, the one named last changes fastest.
Arguments:
- queries: bfloat16 [65536, 1024], P(('dp', 'seq')), parts along dimension 0, may hold values from -6 to 6
- keys: bfloat16 [65536, 1024], P(('dp', 'seq')), parts along dimension 0, may hold values from -4 to 4
- values: bfloat16 [65536, 1024], P(('dp', 'seq')), parts along dimension 0, may hold values from -6 to 6
- cotangent: bfloat16 [65536, 1024], P(('dp', 'seq')), parts along dimension 0, may hold values from -6 to 6
- doc_ids: int32 [65536], P(('dp', 'seq')), parts along dimension 0, may hold values from 0 to 15, never falling along the last dimension, each value on 1 to 4096 neighbouring positions
Outputs:
- attended: bfloat16 [65536, 1024], P(('dp', 'seq')), parts along dimension 0
- grad_queries: bfloat16 [65536, 1024], P(('dp', 'seq')), parts along dimension 0
- grad_keys: bfloat16 [65536, 1024], P(('dp', 'seq')), parts along dimension 0
- grad_values: bfloat16 [65536, 1024], P(('dp', 'seq')), parts along dimension 0
There are 8 independent parts, one for each index of `dp`. A program takes and returns all parts, laid end to end along the dimension named above; each array names one. Nothing has to cross between parts.
Inputs may be any that keep to these rules, and one draw needn't show every extreme that they name: doc_ids never fall along the sequence; each document holds 1 to 4096 positions.
All inputs are finite; a program needn't handle non-finite values.
Results may differ from a plain program's by a relative error of at most 0.0058.
Values may be sent and summed in bfloat16 or wider, within the bound.
A program may use at most 128 MiB of HBM per device.

v0:
```python
import jax
import jax.numpy as jnp
import numpy as np
from jax import lax
from jax.sharding import PartitionSpec as P

H = 8
HD = 128
SEG = 1024
LEVELS = 2


MASKED = -1e30


def for_sending(shard):
    return jax.tree.map(lambda a: a.astype(jnp.bfloat16) if a.dtype == jnp.float32 else a, shard)


def from_partner(shard, axis, stride):
    return lax.ppermute(shard, axis, [(i, i ^ 1 << stride) for i in range(lax.axis_size(axis))])


def dilate(array, dilation_step):
    heads = array.shape[1]
    rows = array.shape[0] // dilation_step
    shaped = array.reshape((rows, dilation_step) + array.shape[1:])
    return shaped[:, np.arange(heads) % dilation_step, np.arange(heads)]


def place_rows(array, dilation_step, filler):
    heads = array.shape[1]
    rows = array.shape[0]
    empty = jnp.full((rows, dilation_step) + array.shape[1:], filler, array.dtype)
    filled = empty.at[:, np.arange(heads) % dilation_step, np.arange(heads)].set(array)
    return filled.reshape((rows * dilation_step,) + array.shape[1:])


def block_order(group_rank, bit_total, rows_sel):
    blocks = jnp.reshape(group_rank, (1,))
    for bit_index in range(bit_total):
        blocks = jnp.concatenate([blocks, blocks ^ 1 << bit_index], 0)
    offsets = jnp.arange(rows_sel, dtype=jnp.int32)
    return (blocks[:, None] * rows_sel + offsets[None, :]).reshape(-1)


def join_pair(own_rows, their_rows):
    return tuple(
        (
            jnp.concatenate([own_part, their_part], 0)
            for own_part, their_part in zip(own_rows, their_rows)
        )
    )


def swap_keys_apart(parts, bit_index):
    return tuple(from_partner((parts[0], parts[1], for_sending(parts[2])), "seq", bit_index))


def swap_queries_apart(parts, bit_index):
    big_part = from_partner((parts[0], parts[1]), "seq", bit_index)
    small_part = from_partner((parts[2], parts[3], parts[4]), "seq", bit_index)
    return tuple(big_part) + tuple(small_part)


def spread_rows(bundle, bit_total, swapper):
    for bit_index in range(bit_total):
        received = swapper(bundle, bit_index)
        bundle = join_pair(bundle, received)
    return bundle


def level_scores(query_sel, key_sel, query_docs, key_docs, query_pos, key_pos):
    score = jnp.einsum(
        "ihd,jhd->hij", query_sel, key_sel, preferred_element_type=jnp.float32
    ) * HD ** (-0.5)
    allowed = (key_pos[None, None, :] <= query_pos[None, :, None]) & (
        query_docs.T[:, :, None] == key_docs.T[:, None, :]
    )
    return jnp.where(allowed, score, MASKED)


def per_device(queries, keys, values, cotangent, doc_ids):
    tokens_here = queries.shape[0]
    shape_three = (tokens_here, H, HD)
    score_scale = HD ** (-0.5)
    query_rows = queries.reshape(shape_three)
    key_rows = keys.reshape(shape_three)
    value_rows = values.reshape(shape_three)
    grad_rows = cotangent.reshape(shape_three)
    doc_heads = jnp.broadcast_to(doc_ids[:, None], (tokens_here, H))
    device_rank = lax.axis_index("seq")
    finest = tokens_here * lax.axis_size("seq") // (2 * SEG)
    dilations = [finest * 2**index_of_level for index_of_level in range(LEVELS)]
    level_bits = [
        (SEG * dilations[index_of_level] // tokens_here).bit_length() - 1
        for index_of_level in range(LEVELS)
    ]
    own_query = []
    own_key = []
    bundles = []
    own_pos = []
    group_pos = []
    for index_of_level in range(LEVELS):
        dilation_step = dilations[index_of_level]
        docs_sel = dilate(doc_heads, dilation_step)
        key_sel = dilate(key_rows, dilation_step)
        value_sel = dilate(value_rows, dilation_step)
        own_query.append((dilate(query_rows, dilation_step), docs_sel))
        own_key.append((key_sel, value_sel))
        bundles.append((key_sel, value_sel, docs_sel))
        rows_sel = key_sel.shape[0]
        group_rank = device_rank % 2 ** level_bits[index_of_level]
        own_pos.append(group_rank * rows_sel + jnp.arange(rows_sel, dtype=jnp.int32))
        group_pos.append(block_order(group_rank, level_bits[index_of_level], rows_sel))
    bundles = [
        spread_rows(bundles[index_of_level], level_bits[index_of_level], swap_keys_apart)
        for index_of_level in range(LEVELS)
    ]
    lse_full = []
    part_full = []
    saved = []
    for index_of_level in range(LEVELS):
        dilation_step = dilations[index_of_level]
        query_sel, query_docs = own_query[index_of_level]
        key_group, value_group, key_docs = bundles[index_of_level]
        score = level_scores(
            query_sel,
            key_group,
            query_docs,
            key_docs,
            own_pos[index_of_level],
            group_pos[index_of_level],
        )
        top_score = jnp.max(score, -1)
        log_total = top_score + jnp.log(jnp.sum(jnp.exp(score - top_score[..., None]), -1))
        probs = jnp.exp(score - log_total[..., None]).astype(jnp.bfloat16)
        attended = jnp.einsum(
            "hij,jhd->ihd", probs, value_group, preferred_element_type=jnp.float32
        )
        lse_full.append(place_rows(log_total.T, dilation_step, MASKED))
        part_full.append(place_rows(attended, dilation_step, 0.0))
        saved.append(log_total)
    top_level = lse_full[0]
    index_of_level = 1
    top_level = jnp.maximum(top_level, lse_full[index_of_level])
    level_total = jnp.zeros_like(top_level)
    for index_of_level in range(LEVELS):
        level_total = level_total + jnp.exp(lse_full[index_of_level] - top_level)
    merged_log = top_level + jnp.log(level_total)
    weight_matrix = [jnp.exp(entry_lse - merged_log) for entry_lse in lse_full]
    combined = jnp.zeros(shape_three, jnp.float32)
    for index_of_level in range(LEVELS):
        combined = combined + weight_matrix[index_of_level][..., None] * part_full[index_of_level]
    dot_sum = jnp.sum(grad_rows.astype(jnp.float32) * combined, -1)
    grad_query = jnp.zeros(shape_three, jnp.float32)
    requests = []
    for index_of_level in range(LEVELS):
        dilation_step = dilations[index_of_level]
        query_sel, query_docs = own_query[index_of_level]
        key_group, value_group, key_docs = bundles[index_of_level]
        weight_sel = dilate(weight_matrix[index_of_level], dilation_step)
        dot_sel = dilate(dot_sum, dilation_step)
        dout_sel = dilate(grad_rows, dilation_step)
        score = level_scores(
            query_sel,
            key_group,
            query_docs,
            key_docs,
            own_pos[index_of_level],
            group_pos[index_of_level],
        )
        probs = jnp.exp(score - saved[index_of_level][..., None])
        dprob = jnp.einsum(
            "ihd,jhd->hij", dout_sel, value_group, preferred_element_type=jnp.float32
        )
        gain = weight_sel.T[:, :, None]
        dscore = (gain * probs * (dprob - dot_sel.T[:, :, None])).astype(jnp.bfloat16)
        level_queries = (
            jnp.einsum("hij,jhd->ihd", dscore, key_group, preferred_element_type=jnp.float32)
            * score_scale
        )
        grad_query = grad_query + place_rows(level_queries, dilation_step, 0.0)
        requests.append((query_sel, dout_sel, saved[index_of_level].T, weight_sel, dot_sel))
    groups = [
        spread_rows(requests[index_of_level], level_bits[index_of_level], swap_queries_apart)
        for index_of_level in range(LEVELS)
    ]
    grad_key = jnp.zeros(shape_three, jnp.float32)
    grad_value = jnp.zeros(shape_three, jnp.float32)
    for index_of_level in range(LEVELS):
        dilation_step = dilations[index_of_level]
        query_group, dout_group, lse_group, weight_group, dot_group = groups[index_of_level]
        key_sel, value_sel = own_key[index_of_level]
        own_docs = own_query[index_of_level][1]
        group_docs = bundles[index_of_level][2]
        score = level_scores(
            query_group,
            key_sel,
            group_docs,
            own_docs,
            group_pos[index_of_level],
            own_pos[index_of_level],
        )
        probs = jnp.exp(score - lse_group.T[:, :, None])
        dprob = jnp.einsum(
            "ihd,jhd->hij", dout_group, value_sel, preferred_element_type=jnp.float32
        )
        gain = weight_group.T[:, :, None]
        dscore = (gain * probs * (dprob - dot_group.T[:, :, None])).astype(jnp.bfloat16)
        weighted = (gain * probs).astype(jnp.bfloat16)
        level_k = (
            jnp.einsum("hij,ihd->jhd", dscore, query_group, preferred_element_type=jnp.float32)
            * score_scale
        )
        level_v = jnp.einsum(
            "hij,ihd->jhd", weighted, dout_group, preferred_element_type=jnp.float32
        )
        grad_key = grad_key + place_rows(level_k, dilation_step, 0.0)
        grad_value = grad_value + place_rows(level_v, dilation_step, 0.0)
    flattened_shape = (tokens_here, H * HD)
    return (
        combined.astype(jnp.bfloat16).reshape(flattened_shape),
        grad_query.astype(jnp.bfloat16).reshape(flattened_shape),
        grad_key.astype(jnp.bfloat16).reshape(flattened_shape),
        grad_value.astype(jnp.bfloat16).reshape(flattened_shape),
    )


def solution(mesh):
    in_specs = (
        P(("dp", "seq"), None),
        P(("dp", "seq"), None),
        P(("dp", "seq"), None),
        P(("dp", "seq"), None),
        P(("dp", "seq")),
    )
    out_specs = (
        P(("dp", "seq"), None),
        P(("dp", "seq"), None),
        P(("dp", "seq"), None),
        P(("dp", "seq"), None),
    )
    return jax.shard_map(
        per_device, mesh=mesh, in_specs=in_specs, out_specs=out_specs, check_vma=False
    )
```

profile of v0, /device:TPU:1, one launch (start us, length us, event | category | flops | bytes accessed | tf_op | source)
XLA Modules:
  0.0 896.2 jit_solution(9088878963195117615)
XLA Ops:
  3.1 8.8 collective-permute-start.16
  48.9 4.9 collective-permute-start.2
  55.8 3.4 collective-permute-start.3
  62.6 4.2 collective-permute-start.4
  70.6 5.0 collective-permute-start.5
  76.3 4.3 collective-permute-start.76
  95.5 3.4 collective-permute-start.28
  101.7 3.4 collective-permute-start.59
  118.2 3.4 collective-permute-start.34
  126.8 4.2 collective-permute-start.29
  134.7 4.2 collective-permute-start.60
  142.9 4.1 collective-permute-start.7
  152.2 4.1 collective-permute-start.35
  160.7 3.4 collective-permute-start.30
  167.0 3.4 collective-permute-start.61
  173.7 3.4 collective-permute-start.25
  185.4 7.1 collective-permute-done.8
  194.7 4.3 collective-permute-start.9
  199.9 20.2 %collective-permute-done.25 = bf16[256,8,128]{2,0,1:T(8,128)(2,1)S(1)} collective-permute-done((bf16[256,8,128]{2,0,1:T(8,128)(2,1)S(1)}, bf16[256,8,128]{2,0,1:T(8,128)(2,1)S(1)}, u32[]{:S(2)}, u32[]{:S(2)}) %collective-permute-start.25) | collective-permute-done | bytes 524320 | tf_op jit(solution)/shard_map/ppermute | solution.py:21
  222.4 15.0 %collective-permute-done.51 = bf16[256,8,128]{2,0,1:T(8,128)(2,1)S(1)} collective-permute-done((bf16[256,8,128]{2,0,1:T(8,128)(2,1)S(1)}, bf16[256,8,128]{2,0,1:T(8,128)(2,1)S(1)}, u32[]{:S(2)}, u32[]{:S(2)}) %collective-permute-start.51) | collective-permute-done | bytes 524320 | tf_op jit(solution)/shard_map/ppermute | solution.py:21
  237.4 5.7 collective-permute-start.80
  244.3 4.3 collective-permute-done.36
  248.6 5.7 collective-permute-start.62
  257.8 102.6 %collective-permute-done.31 = bf16[256,8,128]{2,0,1:T(8,128)(2,1)S(1)} collective-permute-done((bf16[256,8,128]{2,0,1:T(8,128)(2,1)S(1)}, bf16[256,8,128]{2,0,1:T(8,128)(2,1)S(1)}, u32[]{:S(2)}, u32[]{:S(2)}) %collective-permute-start.31) | collective-permute-done | bytes 524320 | tf_op jit(solution)/shard_map/ppermute | solution.py:21
  363.5 154.2 %collective-permute-done.80 = bf16[256,8,128]{2,0,1:T(8,128)(2,1)S(1)} collective-permute-done((bf16[256,8,128]{2,0,1:T(8,128)(2,1)S(1)}, bf16[256,8,128]{2,0,1:T(8,128)(2,1)S(1)}, u32[]{:S(2)}, u32[]{:S(2)}) %collective-permute-start.80) | collective-permute-done | bytes 524320 | tf_op jit(solution)/shard_map/ppermute | solution.py:21
  520.9 8.1 collective-permute-done.62
  532.1 7.4 collective-permute-start.32
  541.1 10.3 %collective-permute-done.26 = bf16[512,8,128]{2,0,1:T(8,128)(2,1)S(1)} collective-permute-done((bf16[512,8,128]{2,0,1:T(8,128)(2,1)S(1)}, bf16[512,8,128]{2,0,1:T(8,128)(2,1)S(1)}, u32[]{:S(2)}, u32[]{:S(2)}) %collective-permute-start.26) | collective-permute-done | bytes 1048608 | tf_op jit(solution)/shard_map/ppermute | solution.py:21
  551.4 32.1 %collective-permute-start.43 = (f32[32,8]{0,1:T(8,128)S(1)}, f32[32,8]{0,1:T(8,128)S(1)}, u32[]{:S(2)}, u32[]{:S(2)}) collective-permute-start(f32[32,8]{0,1:T(8,128)S(1)} %bitcast.280), channel_id=1, source_target_pairs={{0,8},{8,0},{16,24},{24,16},{32,40},{40,32},{48,56},{56,48},{64,72... | collective-permute-start | bytes 3080 | tf_op jit(solution)/shard_map/ppermute | solution.py:21
  592.1 4.4 collective-permute-done.37
  596.5 5.5 collective-permute-start.45
  606.8 66.3 %collective-permute-done.46 = f32[256,8]{0,1:T(8,128)S(1)} collective-permute-done((f32[256,8]{0,1:T(8,128)S(1)}, f32[256,8]{0,1:T(8,128)S(1)}, u32[]{:S(2)}, u32[]{:S(2)}) %collective-permute-start.46) | collective-permute-done | bytes 8224 | tf_op jit(solution)/shard_map/ppermute | solution.py:21
  673.1 6.7 collective-permute-start.63
  691.7 11.8 %collective-permute-done.47 = f32[512,8]{0,1:T(8,128)} collective-permute-done((f32[512,8]{0,1:T(8,128)}, f32[512,8]{0,1:T(8,128)}, u32[]{:S(2)}, u32[]{:S(2)}) %collective-permute-start.47) | collective-permute-done | bytes 16416 | tf_op jit(solution)/shard_map/ppermute | solution.py:21
  740.7 35.3 %collective-permute-start.70 = (f32[16,8]{0,1:T(8,128)S(1)}, f32[16,8]{0,1:T(8,128)S(1)}, u32[]{:S(2)}, u32[]{:S(2)}) collective-permute-start(f32[16,8]{0,1:T(8,128)S(1)} %bitcast.273), channel_id=1, source_target_pairs={{0,8},{8,0},{16,24},{24,16},{32,40},{40,32},{48,56},{56,48},{64,72... | collective-permute-start | bytes 1544 | tf_op jit(solution)/shard_map/ppermute | solution.py:21
  787.9 5.2 collective-permute-start.71
  804.1 3.8 collective-permute-start.72
  811.0 3.8 collective-permute-start.84
  818.0 3.8 collective-permute-start.55
  823.9 3.4 collective-permute-start.67
  829.3 3.4 collective-permute-start.41
  836.5 6.4 collective-permute-start.74
  845.0 4.3 collective-permute-start.86
  851.4 4.3 collective-permute-start.57
  858.7 5.0 collective-permute-start.75
  864.4 4.2 collective-permute-start.69
  869.3 5.0 collective-permute-start.87
  874.5 3.7 fusion.13
  (520 shorter events, 262.7 us)
Async XLA Ops:
  3.1 78.2 %collective-permute-start.16 = (bf16[16,8,128]{2,0,1:T(8,128)(2,1)}, bf16[16,8,128]{2,0,1:T(8,128)(2,1)}, u32[]{:S(2)}, u32[]{:S(2)}) collective-permute-start(bf16[16,8,128]{2,0,1:T(8,128)(2,1)} %bitcast.12), channel_id=1, source_target_pairs={{0,8},{8,0},{16,24},{24,16},{32,40},{40,32},{48,56},{56,48},{64,72... | collective-permute-start | bytes 98312 | tf_op jit(solution)/shard_map/ppermute | solution.py:21
  13.6 72.0 %collective-permute-start.27 = (bf16[16,8,128]{2,0,1:T(8,128)(2,1)S(1)}, bf16[16,8,128]{2,0,1:T(8,128)(2,1)}, u32[]{:S(2)}, u32[]{:S(2)}) collective-permute-start(bf16[16,8,128]{2,0,1:T(8,128)(2,1)S(1)} %bitcast.228), channel_id=1, source_target_pairs={{0,8},{8,0},{16,24},{24,16},{32,40},{40,32},{48,56},{56,48},{64,72... | collective-permute-start | bytes 98312 | tf_op jit(solution)/shard_map/ppermute | solution.py:21
  16.3 25.0 %collective-permute-start.10 = (s32[16,8]{0,1:T(8,128)S(1)}, s32[16,8]{0,1:T(8,128)S(1)}, u32[]{:S(2)}, u32[]{:S(2)}) collective-permute-start(s32[16,8]{0,1:T(8,128)S(1)} %bitcast.254), channel_id=1, source_target_pairs={{0,8},{8,0},{16,24},{24,16},{32,40},{40,32},{48,56},{56,48},{64,72... | collective-permute-start | bytes 1544 | tf_op jit(solution)/shard_map/ppermute | solution.py:21
  19.4 76.0 %collective-permute-start.22 = (bf16[32,8,128]{2,0,1:T(8,128)(2,1)S(1)}, bf16[32,8,128]{2,0,1:T(8,128)(2,1)}, u32[]{:S(2)}, u32[]{:S(2)}) collective-permute-start(bf16[32,8,128]{2,0,1:T(8,128)(2,1)S(1)} %bitcast.224), channel_id=1, source_target_pairs={{0,8},{8,0},{16,24},{24,16},{32,40},{40,32},{48,56},{56,48},{64,72... | collective-permute-start | bytes 196616 | tf_op jit(solution)/shard_map/ppermute | solution.py:21
  22.1 21.2 %collective-permute-start = (s32[32,8]{0,1:T(8,128)S(1)}, s32[32,8]{0,1:T(8,128)S(1)}, u32[]{:S(2)}, u32[]{:S(2)}) collective-permute-start(s32[32,8]{0,1:T(8,128)S(1)} %bitcast.248), channel_id=1, source_target_pairs={{0,8},{8,0},{16,24},{24,16},{32,40},{40,32},{48,56},{56,48},{64,72... | collective-permute-start | bytes 3080 | tf_op jit(solution)/shard_map/ppermute | solution.py:21
  70.6 29.1 %collective-permute-start.5 = (bf16[32,8,128]{2,0,1:T(8,128)(2,1)S(1)}, bf16[32,8,128]{2,0,1:T(8,128)(2,1)S(1)}, u32[]{:S(2)}, u32[]{:S(2)}) collective-permute-start(bf16[32,8,128]{2,0,1:T(8,128)(2,1)S(1)} %bitcast.210), channel_id=1, source_target_pairs={{0,8},{8,0},{16,24},{24,16},{32,40},{40,32},{48,56},{56,48},{64,72... | collective-permute-start | bytes 196616 | tf_op jit(solution)/shard_map/ppermute | solution.py:21
  95.5 19.2 %collective-permute-start.28 = (bf16[32,8,128]{2,0,1:T(8,128)(2,1)S(1)}, bf16[32,8,128]{2,0,1:T(8,128)(2,1)S(1)}, u32[]{:S(2)}, u32[]{:S(2)}) collective-permute-start(bf16[32,8,128]{2,0,1:T(8,128)(2,1)S(1)} %pad_maximum_fusion.21), channel_id=1, source_target_pairs={{0,16},{8,24},{16,0},{24,8},{32,48},{40,56},{48,32},{56,40},{64,80... | collective-permute-start | bytes 196616 | tf_op jit(solution)/shard_map/ppermute | solution.py:21
  101.7 21.4 %collective-permute-start.59 = (bf16[32,8,128]{2,0,1:T(8,128)(2,1)S(1)}, bf16[32,8,128]{2,0,1:T(8,128)(2,1)S(1)}, u32[]{:S(2)}, u32[]{:S(2)}) collective-permute-start(bf16[32,8,128]{2,0,1:T(8,128)(2,1)S(1)} %pad_maximum_fusion.22), channel_id=1, source_target_pairs={{0,16},{8,24},{16,0},{24,8},{32,48},{40,56},{48,32},{56,40},{64,80... | collective-permute-start | bytes 196616 | tf_op jit(solution)/shard_map/ppermute | solution.py:21
  105.1 21.7 %collective-permute-start.23 = (bf16[64,8,128]{2,0,1:T(8,128)(2,1)S(1)}, bf16[64,8,128]{2,0,1:T(8,128)(2,1)S(1)}, u32[]{:S(2)}, u32[]{:S(2)}) collective-permute-start(bf16[64,8,128]{2,0,1:T(8,128)(2,1)S(1)} %pad_maximum_fusion.14), channel_id=1, source_target_pairs={{0,16},{8,24},{16,0},{24,8},{32,48},{40,56},{48,32},{56,40},{64,80... | collective-permute-start | bytes 393224 | tf_op jit(solution)/shard_map/ppermute | solution.py:21
  110.6 21.4 %collective-permute-start.6 = (bf16[64,8,128]{2,0,1:T(8,128)(2,1)S(1)}, bf16[64,8,128]{2,0,1:T(8,128)(2,1)S(1)}, u32[]{:S(2)}, u32[]{:S(2)}) collective-permute-start(bf16[64,8,128]{2,0,1:T(8,128)(2,1)S(1)} %pad_maximum_fusion.12), channel_id=1, source_target_pairs={{0,16},{8,24},{16,0},{24,8},{32,48},{40,56},{48,32},{56,40},{64,80... | collective-permute-start | bytes 393224 | tf_op jit(solution)/shard_map/ppermute | solution.py:21
  114.7 20.0 %collective-permute-start.49 = (bf16[64,8,128]{2,0,1:T(8,128)(2,1)S(1)}, bf16[64,8,128]{2,0,1:T(8,128)(2,1)S(1)}, u32[]{:S(2)}, u32[]{:S(2)}) collective-permute-start(bf16[64,8,128]{2,0,1:T(8,128)(2,1)S(1)} %pad_maximum_fusion.17), channel_id=1, source_target_pairs={{0,16},{8,24},{16,0},{24,8},{32,48},{40,56},{48,32},{56,40},{64,80... | collective-permute-start | bytes 393224 | tf_op jit(solution)/shard_map/ppermute | solution.py:21
  118.2 20.8 %collective-permute-start.34 = (bf16[64,8,128]{2,0,1:T(8,128)(2,1)S(1)}, bf16[64,8,128]{2,0,1:T(8,128)(2,1)S(1)}, u32[]{:S(2)}, u32[]{:S(2)}) collective-permute-start(bf16[64,8,128]{2,0,1:T(8,128)(2,1)S(1)} %pad_maximum_fusion.16), channel_id=1, source_target_pairs={{0,16},{8,24},{16,0},{24,8},{32,48},{40,56},{48,32},{56,40},{64,80... | collective-permute-start | bytes 393224 | tf_op jit(solution)/shard_map/ppermute | solution.py:21
  123.1 19.8 %collective-permute-start.18 = (bf16[64,8,128]{2,0,1:T(8,128)(2,1)S(1)}, bf16[64,8,128]{2,0,1:T(8,128)(2,1)S(1)}, u32[]{:S(2)}, u32[]{:S(2)}) collective-permute-start(bf16[64,8,128]{2,0,1:T(8,128)(2,1)S(1)} %pad_maximum_fusion.13), channel_id=1, source_target_pairs={{0,32},{8,40},{16,48},{24,56},{32,0},{40,8},{48,16},{56,24},{64,96... | collective-permute-start | bytes 393224 | tf_op jit(solution)/shard_map/ppermute | solution.py:21
  126.8 21.0 %collective-permute-start.29 = (bf16[64,8,128]{2,0,1:T(8,128)(2,1)S(1)}, bf16[64,8,128]{2,0,1:T(8,128)(2,1)S(1)}, u32[]{:S(2)}, u32[]{:S(2)}) collective-permute-start(bf16[64,8,128]{2,0,1:T(8,128)(2,1)S(1)} %pad_maximum_fusion.15), channel_id=1, source_target_pairs={{0,32},{8,40},{16,48},{24,56},{32,0},{40,8},{48,16},{56,24},{64,96... | collective-permute-start | bytes 393224 | tf_op jit(solution)/shard_map/ppermute | solution.py:21
  131.9 20.2 %collective-permute-start.78 = (bf16[64,8,128]{2,0,1:T(8,128)(2,1)S(1)}, bf16[64,8,128]{2,0,1:T(8,128)(2,1)S(1)}, u32[]{:S(2)}, u32[]{:S(2)}) collective-permute-start(bf16[64,8,128]{2,0,1:T(8,128)(2,1)S(1)} %pad_maximum_fusion.19), channel_id=1, source_target_pairs={{0,32},{8,40},{16,48},{24,56},{32,0},{40,8},{48,16},{56,24},{64,96... | collective-permute-start | bytes 393224 | tf_op jit(solution)/shard_map/ppermute | solution.py:21
  134.7 22.4 %collective-permute-start.60 = (bf16[64,8,128]{2,0,1:T(8,128)(2,1)S(1)}, bf16[64,8,128]{2,0,1:T(8,128)(2,1)S(1)}, u32[]{:S(2)}, u32[]{:S(2)}) collective-permute-start(bf16[64,8,128]{2,0,1:T(8,128)(2,1)S(1)} %pad_maximum_fusion.18), channel_id=1, source_target_pairs={{0,32},{8,40},{16,48},{24,56},{32,0},{40,8},{48,16},{56,24},{64,96... | collective-permute-start | bytes 393224 | tf_op jit(solution)/shard_map/ppermute | solution.py:21
  139.0 21.7 %collective-permute-start.24 = (bf16[128,8,128]{2,0,1:T(8,128)(2,1)S(1)}, bf16[128,8,128]{2,0,1:T(8,128)(2,1)S(1)}, u32[]{:S(2)}, u32[]{:S(2)}) collective-permute-start(bf16[128,8,128]{2,0,1:T(8,128)(2,1)S(1)} %pad_maximum_fusion.6), channel_id=1, source_target_pairs={{0,32},{8,40},{16,48},{24,56},{32,0},{40,8},{48,16},{56,24},{64,96... | collective-permute-start | bytes 786440 | tf_op jit(solution)/shard_map/ppermute | solution.py:21
  142.9 22.1 %collective-permute-start.7 = (bf16[128,8,128]{2,0,1:T(8,128)(2,1)S(1)}, bf16[128,8,128]{2,0,1:T(8,128)(2,1)S(1)}, u32[]{:S(2)}, u32[]{:S(2)}) collective-permute-start(bf16[128,8,128]{2,0,1:T(8,128)(2,1)S(1)} %pad_maximum_fusion.4), channel_id=1, source_target_pairs={{0,32},{8,40},{16,48},{24,56},{32,0},{40,8},{48,16},{56,24},{64,96... | collective-permute-start | bytes 786440 | tf_op jit(solution)/shard_map/ppermute | solution.py:21
  147.8 19.1 %collective-permute-start.50 = (bf16[128,8,128]{2,0,1:T(8,128)(2,1)S(1)}, bf16[128,8,128]{2,0,1:T(8,128)(2,1)S(1)}, u32[]{:S(2)}, u32[]{:S(2)}) collective-permute-start(bf16[128,8,128]{2,0,1:T(8,128)(2,1)S(1)} %pad_maximum_fusion.9), channel_id=1, source_target_pairs={{0,32},{8,40},{16,48},{24,56},{32,0},{40,8},{48,16},{56,24},{64,96... | collective-permute-start | bytes 786440 | tf_op jit(solution)/shard_map/ppermute | solution.py:21
  167.0 27.7 %collective-permute-start.61 = (bf16[128,8,128]{2,0,1:T(8,128)(2,1)S(1)}, bf16[128,8,128]{2,0,1:T(8,128)(2,1)S(1)}, u32[]{:S(2)}, u32[]{:S(2)}) collective-permute-start(bf16[128,8,128]{2,0,1:T(8,128)(2,1)S(1)} %pad_maximum_fusion.10), channel_id=1, source_target_pairs={{0,64},{8,72},{16,80},{24,88},{32,96},{40,104},{48,112},{56,120},{... | collective-permute-start | bytes 786440 | tf_op jit(solution)/shard_map/ppermute | solution.py:21
  170.4 22.1 %collective-permute-start.8 = (bf16[256,8,128]{2,0,1:T(8,128)(2,1)S(1)}, bf16[256,8,128]{2,0,1:T(8,128)(2,1)S(1)}, u32[]{:S(2)}, u32[]{:S(2)}) collective-permute-start(bf16[256,8,128]{2,0,1:T(8,128)(2,1)S(1)} %pad_maximum_fusion), channel_id=1, source_target_pairs={{0,64},{8,72},{16,80},{24,88},{32,96},{40,104},{48,112},{56,120},{... | collective-permute-start | bytes 1572872 | tf_op jit(solution)/shard_map/ppermute | solution.py:21
  173.7 46.4 %collective-permute-start.25 = (bf16[256,8,128]{2,0,1:T(8,128)(2,1)S(1)}, bf16[256,8,128]{2,0,1:T(8,128)(2,1)S(1)}, u32[]{:S(2)}, u32[]{:S(2)}) collective-permute-start(bf16[256,8,128]{2,0,1:T(8,128)(2,1)S(1)} %pad_maximum_fusion.1), channel_id=1, source_target_pairs={{0,64},{8,72},{16,80},{24,88},{32,96},{40,104},{48,112},{56,120},{... | collective-permute-start | bytes 1572872 | tf_op jit(solution)/shard_map/ppermute | solution.py:21
  178.1 59.3 %collective-permute-start.51 = (bf16[256,8,128]{2,0,1:T(8,128)(2,1)S(1)}, bf16[256,8,128]{2,0,1:T(8,128)(2,1)S(1)}, u32[]{:S(2)}, u32[]{:S(2)}) collective-permute-start(bf16[256,8,128]{2,0,1:T(8,128)(2,1)S(1)} %pad_maximum_fusion.3), channel_id=1, source_target_pairs={{0,64},{8,72},{16,80},{24,88},{32,96},{40,104},{48,112},{56,120},{... | collective-permute-start | bytes 1572872 | tf_op jit(solution)/shard_map/ppermute | solution.py:21
  181.0 67.6 %collective-permute-start.36 = (bf16[256,8,128]{2,0,1:T(8,128)(2,1)S(1)}, bf16[256,8,128]{2,0,1:T(8,128)(2,1)S(1)}, u32[]{:S(2)}, u32[]{:S(2)}) collective-permute-start(bf16[256,8,128]{2,0,1:T(8,128)(2,1)S(1)} %pad_maximum_fusion.2), channel_id=1, source_target_pairs={{0,64},{8,72},{16,80},{24,88},{32,96},{40,104},{48,112},{56,120},{... | collective-permute-start | bytes 1572872 | tf_op jit(solution)/shard_map/ppermute | solution.py:21
  192.5 62.1 %collective-permute-start.20 = (bf16[256,8,128]{2,0,1:T(8,128)(2,1)S(1)}, bf16[256,8,128]{2,0,1:T(8,128)(2,1)S(1)}, u32[]{:S(2)}, u32[]{:S(2)}) collective-permute-start(bf16[256,8,128]{2,0,1:T(8,128)(2,1)S(1)} %get-tuple-element.46), channel_id=1, source_target_pairs={{0,128},{8,136},{16,144},{24,152},{32,160},{40,168},{48,176},{56,1... | collective-permute-start | bytes 1572872 | tf_op jit(solution)/shard_map/ppermute | solution.py:21
  194.7 337.4 %collective-permute-start.9 = (bf16[512,8,128]{2,0,1:T(8,128)(2,1)S(1)}, bf16[512,8,128]{2,0,1:T(8,128)(2,1)S(1)}, u32[]{:S(2)}, u32[]{:S(2)}) collective-permute-start(bf16[512,8,128]{2,0,1:T(8,128)(2,1)S(1)} %get-tuple-element.16), channel_id=1, source_target_pairs={{0,128},{8,136},{16,144},{24,152},{32,160},{40,168},{48,176},{56,1... | collective-permute-start | bytes 3145736 | tf_op jit(solution)/shard_map/ppermute | solution.py:21
  220.2 140.2 %collective-permute-start.31 = (bf16[256,8,128]{2,0,1:T(8,128)(2,1)S(1)}, bf16[256,8,128]{2,0,1:T(8,128)(2,1)S(1)}, u32[]{:S(2)}, u32[]{:S(2)}) collective-permute-start(bf16[256,8,128]{2,0,1:T(8,128)(2,1)S(1)} %get-tuple-element.49), channel_id=1, source_target_pairs={{0,128},{8,136},{16,144},{24,152},{32,160},{40,168},{48,176},{56,1... | collective-permute-start | bytes 1572872 | tf_op jit(solution)/shard_map/ppermute | solution.py:21
  237.4 280.4 %collective-permute-start.80 = (bf16[256,8,128]{2,0,1:T(8,128)(2,1)S(1)}, bf16[256,8,128]{2,0,1:T(8,128)(2,1)S(1)}, u32[]{:S(2)}, u32[]{:S(2)}) collective-permute-start(bf16[256,8,128]{2,0,1:T(8,128)(2,1)S(1)} %get-tuple-element.28), channel_id=1, source_target_pairs={{0,128},{8,136},{16,144},{24,152},{32,160},{40,168},{48,176},{56,1... | collective-permute-start | bytes 1572872 | tf_op jit(solution)/shard_map/ppermute | solution.py:21
  248.6 280.4 %collective-permute-start.62 = (bf16[256,8,128]{2,0,1:T(8,128)(2,1)S(1)}, bf16[256,8,128]{2,0,1:T(8,128)(2,1)S(1)}, u32[]{:S(2)}, u32[]{:S(2)}) collective-permute-start(bf16[256,8,128]{2,0,1:T(8,128)(2,1)S(1)} %get-tuple-element.31), channel_id=1, source_target_pairs={{0,128},{8,136},{16,144},{24,152},{32,160},{40,168},{48,176},{56,1... | collective-permute-start | bytes 1572872 | tf_op jit(solution)/shard_map/ppermute | solution.py:21
  254.6 296.8 %collective-permute-start.26 = (bf16[512,8,128]{2,0,1:T(8,128)(2,1)S(1)}, bf16[512,8,128]{2,0,1:T(8,128)(2,1)S(1)}, u32[]{:S(2)}, u32[]{:S(2)}) collective-permute-start(bf16[512,8,128]{2,0,1:T(8,128)(2,1)S(1)} %get-tuple-element.14), channel_id=1, source_target_pairs={{0,128},{8,136},{16,144},{24,152},{32,160},{40,168},{48,176},{56,1... | collective-permute-start | bytes 3145736 | tf_op jit(solution)/shard_map/ppermute | solution.py:21
  360.4 320.2 %collective-permute-start.52 = (bf16[512,8,128]{2,0,1:T(8,128)(2,1)}, bf16[512,8,128]{2,0,1:T(8,128)(2,1)}, u32[]{:S(2)}, u32[]{:S(2)}) collective-permute-start(bf16[512,8,128]{2,0,1:T(8,128)(2,1)} %get-tuple-element.4), channel_id=1, source_target_pairs={{0,128},{8,136},{16,144},{24,152},{32,160},{40,168},{48,176},{56,1... | collective-permute-start | bytes 3145736 | tf_op jit(solution)/shard_map/ppermute | solution.py:21
  517.7 78.8 %collective-permute-start.37 = (bf16[512,8,128]{2,0,1:T(8,128)(2,1)S(1)}, bf16[512,8,128]{2,0,1:T(8,128)(2,1)S(1)}, u32[]{:S(2)}, u32[]{:S(2)}) collective-permute-start(bf16[512,8,128]{2,0,1:T(8,128)(2,1)S(1)} %get-tuple-element.6), channel_id=1, source_target_pairs={{0,128},{8,136},{16,144},{24,152},{32,160},{40,168},{48,176},{56,1... | collective-permute-start | bytes 3145736 | tf_op jit(solution)/shard_map/ppermute | solution.py:21
  529.0 175.9 %collective-permute-start.21 = (bf16[512,8,128]{2,0,1:T(8,128)(2,1)}, bf16[512,8,128]{2,0,1:T(8,128)(2,1)}, u32[]{:S(2)}, u32[]{:S(2)}) collective-permute-start(bf16[512,8,128]{2,0,1:T(8,128)(2,1)} %get-tuple-element.18), channel_id=1, source_target_pairs={{0,256},{8,264},{16,272},{24,280},{32,288},{40,296},{48,304},{56,3... | collective-permute-start | bytes 3145736 | tf_op jit(solution)/shard_map/ppermute | solution.py:21
  532.1 177.9 %collective-permute-start.32 = (bf16[512,8,128]{2,0,1:T(8,128)(2,1)}, bf16[512,8,128]{2,0,1:T(8,128)(2,1)}, u32[]{:S(2)}, u32[]{:S(2)}) collective-permute-start(bf16[512,8,128]{2,0,1:T(8,128)(2,1)} %get-tuple-element.20), channel_id=1, source_target_pairs={{0,256},{8,264},{16,272},{24,280},{32,288},{40,296},{48,304},{56,3... | collective-permute-start | bytes 3145736 | tf_op jit(solution)/shard_map/ppermute | solution.py:21
  551.4 32.9 %collective-permute-start.43 = (f32[32,8]{0,1:T(8,128)S(1)}, f32[32,8]{0,1:T(8,128)S(1)}, u32[]{:S(2)}, u32[]{:S(2)}) collective-permute-start(f32[32,8]{0,1:T(8,128)S(1)} %bitcast.280), channel_id=1, source_target_pairs={{0,8},{8,0},{16,24},{24,16},{32,40},{40,32},{48,56},{56,48},{64,72... | collective-permute-start | bytes 3080 | tf_op jit(solution)/shard_map/ppermute | solution.py:21
  589.1 262.3 %collective-permute-start.81 = (bf16[512,8,128]{2,0,1:T(8,128)(2,1)}, bf16[512,8,128]{2,0,1:T(8,128)(2,1)}, u32[]{:S(2)}, u32[]{:S(2)}) collective-permute-start(bf16[512,8,128]{2,0,1:T(8,128)(2,1)} %get-tuple-element.8), channel_id=1, source_target_pairs={{0,256},{8,264},{16,272},{24,280},{32,288},{40,296},{48,304},{56,3... | collective-permute-start | bytes 3145736 | tf_op jit(solution)/shard_map/ppermute | solution.py:21
  603.1 70.1 %collective-permute-start.46 = (f32[256,8]{0,1:T(8,128)S(1)}, f32[256,8]{0,1:T(8,128)S(1)}, u32[]{:S(2)}, u32[]{:S(2)}) collective-permute-start(f32[256,8]{0,1:T(8,128)S(1)} %pad_maximum_fusion.25), channel_id=1, source_target_pairs={{0,64},{8,72},{16,80},{24,88},{32,96},{40,104},{48,112},{56,120},{... | collective-permute-start | bytes 24584 | tf_op jit(solution)/shard_map/ppermute | solution.py:21
  673.1 109.0 %collective-permute-start.63 = (bf16[512,8,128]{2,0,1:T(8,128)(2,1)}, bf16[512,8,128]{2,0,1:T(8,128)(2,1)}, u32[]{:S(2)}, u32[]{:S(2)}) collective-permute-start(bf16[512,8,128]{2,0,1:T(8,128)(2,1)} %get-tuple-element.10), channel_id=1, source_target_pairs={{0,256},{8,264},{16,272},{24,280},{32,288},{40,296},{48,304},{56,3... | collective-permute-start | bytes 3145736 | tf_op jit(solution)/shard_map/ppermute | solution.py:21
  680.5 23.0 %collective-permute-start.47 = (f32[512,8]{0,1:T(8,128)}, f32[512,8]{0,1:T(8,128)}, u32[]{:S(2)}, u32[]{:S(2)}) collective-permute-start(f32[512,8]{0,1:T(8,128)} %concatenate.560), channel_id=1, source_target_pairs={{0,128},{8,136},{16,144},{24,152},{32,160},{40,168},{48,176},{56,1... | collective-permute-start | bytes 49160 | tf_op jit(solution)/shard_map/ppermute | solution.py:21
  740.7 44.7 %collective-permute-start.70 = (f32[16,8]{0,1:T(8,128)S(1)}, f32[16,8]{0,1:T(8,128)S(1)}, u32[]{:S(2)}, u32[]{:S(2)}) collective-permute-start(f32[16,8]{0,1:T(8,128)S(1)} %bitcast.273), channel_id=1, source_target_pairs={{0,8},{8,0},{16,24},{24,16},{32,40},{40,32},{48,56},{56,48},{64,72... | collective-permute-start | bytes 1544 | tf_op jit(solution)/shard_map/ppermute | solution.py:21
  836.5 21.5 %collective-permute-start.74 = (f32[256,8]{0,1:T(8,128)S(1)}, f32[256,8]{0,1:T(8,128)S(1)}, u32[]{:S(2)}, u32[]{:S(2)}) collective-permute-start(f32[256,8]{0,1:T(8,128)S(1)} %concatenate.588), channel_id=1, source_target_pairs={{0,128},{8,136},{16,144},{24,152},{32,160},{40,168},{48,176},{56,1... | collective-permute-start | bytes 24584 | tf_op jit(solution)/shard_map/ppermute | solution.py:21
  843.0 20.7 %collective-permute-start.68 = (f32[256,8]{0,1:T(8,128)S(1)}, f32[256,8]{0,1:T(8,128)S(1)}, u32[]{:S(2)}, u32[]{:S(2)}) collective-permute-start(f32[256,8]{0,1:T(8,128)S(1)} %concatenate.582), channel_id=1, source_target_pairs={{0,128},{8,136},{16,144},{24,152},{32,160},{40,168},{48,176},{56,1... | collective-permute-start | bytes 24584 | tf_op jit(solution)/shard_map/ppermute | solution.py:21
  845.0 23.6 %collective-permute-start.86 = (f32[256,8]{0,1:T(8,128)S(1)}, f32[256,8]{0,1:T(8,128)S(1)}, u32[]{:S(2)}, u32[]{:S(2)}) collective-permute-start(f32[256,8]{0,1:T(8,128)S(1)} %concatenate.600), channel_id=1, source_target_pairs={{0,128},{8,136},{16,144},{24,152},{32,160},{40,168},{48,176},{56,1... | collective-permute-start | bytes 24584 | tf_op jit(solution)/shard_map/ppermute | solution.py:21
  849.4 25.0 %collective-permute-start.42 = (f32[512,8]{0,1:T(8,128)S(1)}, f32[512,8]{0,1:T(8,128)S(1)}, u32[]{:S(2)}, u32[]{:S(2)}) collective-permute-start(f32[512,8]{0,1:T(8,128)S(1)} %concatenate.555), channel_id=1, source_target_pairs={{0,128},{8,136},{16,144},{24,152},{32,160},{40,168},{48,176},{56,1... | collective-permute-start | bytes 49160 | tf_op jit(solution)/shard_map/ppermute | solution.py:21
  851.4 23.1 %collective-permute-start.57 = (f32[512,8]{0,1:T(8,128)S(1)}, f32[512,8]{0,1:T(8,128)S(1)}, u32[]{:S(2)}, u32[]{:S(2)}) collective-permute-start(f32[512,8]{0,1:T(8,128)S(1)} %concatenate.570), channel_id=1, source_target_pairs={{0,128},{8,136},{16,144},{24,152},{32,160},{40,168},{48,176},{56,1... | collective-permute-start | bytes 49160 | tf_op jit(solution)/shard_map/ppermute | solution.py:21
  858.7 26.1 %collective-permute-start.75 = (f32[512,8]{0,1:T(8,128)}, f32[512,8]{0,1:T(8,128)}, u32[]{:S(2)}, u32[]{:S(2)}) collective-permute-start(f32[512,8]{0,1:T(8,128)} %concatenate.589), channel_id=1, source_target_pairs={{0,256},{8,264},{16,272},{24,280},{32,288},{40,296},{48,304},{56,3... | collective-permute-start | bytes 49160 | tf_op jit(solution)/shard_map/ppermute | solution.py:21
  864.4 21.2 %collective-permute-start.69 = (f32[512,8]{0,1:T(8,128)}, f32[512,8]{0,1:T(8,128)}, u32[]{:S(2)}, u32[]{:S(2)}) collective-permute-start(f32[512,8]{0,1:T(8,128)} %concatenate.583), channel_id=1, source_target_pairs={{0,256},{8,264},{16,272},{24,280},{32,288},{40,296},{48,304},{56,3... | collective-permute-start | bytes 49160 | tf_op jit(solution)/shard_map/ppermute | solution.py:21
  869.3 21.1 %collective-permute-start.87 = (f32[512,8]{0,1:T(8,128)}, f32[512,8]{0,1:T(8,128)}, u32[]{:S(2)}, u32[]{:S(2)}) collective-permute-start(f32[512,8]{0,1:T(8,128)} %concatenate.601), channel_id=1, source_target_pairs={{0,256},{8,264},{16,272},{24,280},{32,288},{40,296},{48,304},{56,3... | collective-permute-start | bytes 49160 | tf_op jit(solution)/shard_map/ppermute | solution.py:21
  (113 other events, 2594.7 us)
where the time goes:
time: 905 us; the launch traced here: 896 us
  waiting for transfers between devices  408 us (45%)
  starting transfers between devices  339 us (37%)
  local copies, waits for them, and re-layouts  99.3 us (11%)
  matrix products  24.4 us (3%)
  other arithmetic  21.7 us (2%)
    ppermute x88, waiting for transfers between devices, from_partner(): lax.ppermute(shard, axis, [(i, i ^ 1 << stride) for i in range(lax.axis_s...  408 us
    ppermute x88, starting transfers between devices, from_partner(): lax.ppermute(shard, axis, [(i, i ^ 1 << stride) for i in range(lax.axis_s...  339 us
    unnamed x187, local copies, waits for them, and re-layouts  32.3 us
    concatenate x36, local copies, waits for them, and re-layouts, join_pair(): jnp.concatenate([own_part, their_part], 0)  25.9 us
    scatter x21, local copies, waits for them, and re-layouts, place_rows(): empty.at[:, np.arange(heads) % dilation_step, np.arange(heads)].set(array)  22.5 us
  transfers between devices with their start and end apart: 88, of which 14 were waited for; matrix products, arithmetic and copies ran while one was open for 15% of the time, Pallas kernels for 0%

commit v1 on v0

v1 whole, which is shorter than its diff:
```python
import jax
import jax.numpy as jnp
from jax import lax
from jax.experimental import pallas as pl
from jax.experimental.pallas import tpu as pltpu
from jax.sharding import PartitionSpec as P

H = 8
HD = 128
SEQ_DEVICES = 64
GROUP = 32
TOKENS = 128
ROWS = 16
SEG_ROWS = GROUP * ROWS
BLOCK = 256
CLASSES = 8
FINEST = 4
SCORE_SCALE = HD**-0.5
LOG2_E = 1.4426950408889634
MASKED = -1e30
MESH_ID = pl.DeviceIdType.MESH

Q_A, Q_B, K_B, V_B, D_A, D_B, K_A, V_A, DOC = range(9)
Q_OF, K_OF, V_OF, D_OF = (Q_A, Q_B), (K_A, K_B), (V_A, V_B), (D_A, D_B)


def dot_nn(a, b):
    return jnp.dot(a, b, preferred_element_type=jnp.float32)


def dot_nt(a, b):
    return lax.dot_general(a, b, (((1,), (1,)), ((), ())), preferred_element_type=jnp.float32)


def iota(shape, dim):
    return lax.broadcasted_iota(jnp.int32, shape, dim)


def one_hot_rows(shape, lane):
    return (iota(shape, 1) == lane).astype(jnp.bfloat16)


def selector(head):
    shape = (2 * ROWS, TOKENS)
    row = iota(shape, 0)
    kind = (head + FINEST * (row >> 4)) & (CLASSES - 1)
    return iota(shape, 1) == CLASSES * (row & (ROWS - 1)) + kind


def worker_of(head, half):
    return GROUP * half + 8 + 2 * head


def exchange_kernel(
    q_hbm, k_hbm, v_hbm, g_hbm, doc_ref, back, backx,
    xin, snd, recv, recvx, res, resx, col, row, kt, vt, sbuf, dpbuf, dkv,
    in_sem, send_sem, recv_sem, recvx_sem, ret_sem, back_sem, backx_sem,
):
    me = lax.axis_index("seq")
    half = me // GROUP
    rank = lax.rem(me, GROUP)
    is_worker = (rank >= 8) & (rank < 24) & (lax.rem(rank, 2) == 0)
    head = (rank - 8) // 2

    loads = [
        pltpu.make_async_copy(ref, xin.at[i], in_sem.at[i])
        for i, ref in enumerate((q_hbm, k_hbm, v_hbm, g_hbm))
    ]
    for load in loads:
        load.start()

    barrier = pltpu.get_barrier_semaphore()

    def greet(device):
        @pl.when(device != me)
        def _():
            pl.semaphore_signal(barrier, inc=1, device_id={"seq": device}, device_id_type=MESH_ID)

    @pl.when(half == 0)
    def _():
        lax.fori_loop(0, H, lambda i, c: (greet(worker_of(i, 0)), c)[1], 0)

    lax.fori_loop(0, H, lambda i, c: (greet(worker_of(i, 1)), c)[1], 0)

    @pl.when(is_worker)
    def _():
        lax.fori_loop(0, GROUP * (1 + half), lambda i, c: (greet(i), c)[1], 0)

    packs = [selector(h) for h in range(H)]
    doc_row = jnp.broadcast_to(doc_ref[...], (2 * ROWS, TOKENS)).astype(jnp.float32)
    ones = jnp.ones((TOKENS, TOKENS), jnp.bfloat16)
    first_lanes = iota((ROWS, HD), 1) < HD // 2
    for h in range(H):
        docs = dot_nn(jnp.where(packs[h], doc_row, 0.0).astype(jnp.bfloat16), ones)
        snd[h, DOC] = jnp.where(first_lanes, docs[:ROWS], docs[ROWS:]).astype(jnp.bfloat16)
    one_hots = [p.astype(jnp.bfloat16) for p in packs]
    for i, (slot_a, slot_b) in enumerate(((Q_A, Q_B), (K_A, K_B), (V_A, V_B), (D_A, D_B))):
        loads[i].wait()
        for h in range(H):
            rows = dot_nn(one_hots[h], xin[i, :, h * HD : (h + 1) * HD]).astype(jnp.bfloat16)
            snd[h, slot_a] = rows[:ROWS]
            snd[h, slot_b] = rows[ROWS:]

    own_sources = jnp.where(is_worker, GROUP * (1 + half) - 1, 0)
    own_workers = jnp.where(half == 0, 2 * H, H) - jnp.where(is_worker, 1, 0)
    pl.semaphore_wait(barrier, own_sources + own_workers)

    place = pl.ds(pl.multiple_of(rank * ROWS, ROWS), ROWS)

    def send_main(h):
        return pltpu.make_async_remote_copy(
            snd.at[h], recv.at[:, place], send_sem, recv_sem,
            device_id={"seq": worker_of(h, half)}, device_id_type=MESH_ID,
        )

    def send_cross(h):
        return pltpu.make_async_remote_copy(
            snd.at[h, pl.ds(K_A, 3)], recvx.at[:, place], send_sem, recvx_sem,
            device_id={"seq": worker_of(h, 1)}, device_id_type=MESH_ID,
        )

    def send_head(i, carry):
        h = lax.rem(i + me, H)
        target = worker_of(h, half)

        @pl.when(target != me)
        def _():
            send_main(h).start()

        @pl.when(target == me)
        def _():
            pltpu.make_async_copy(snd.at[h], recv.at[:, place], recv_sem).start()

        @pl.when(half == 0)
        def _():
            send_cross(h).start()

        return carry

    lax.fori_loop(0, H, send_head, 0)

    @pl.when(is_worker)
    def _():
        @pl.when(half == 0)
        def _():
            recvx[...] = jnp.zeros_like(recvx)

        pltpu.make_async_copy(recv, recv, recv_sem).wait()

        @pl.when(half == 1)
        def _():
            pltpu.make_async_copy(recvx, recvx, recvx_sem).wait()

        attention(head, half, recv, recvx, res, resx, col, row, kt, vt, sbuf, dpbuf, dkv)

        def send_back(i, carry):
            r = lax.rem(i + rank, GROUP)
            target = GROUP * half + r
            rows = pl.ds(pl.multiple_of(r * ROWS, ROWS), ROWS)

            @pl.when(target != me)
            def _():
                pltpu.make_async_remote_copy(
                    res.at[:, rows], back.at[head], ret_sem, back_sem,
                    device_id={"seq": target}, device_id_type=MESH_ID,
                ).start()

            @pl.when(target == me)
            def _():
                pltpu.make_async_copy(res.at[:, rows], back.at[head], back_sem).start()

            @pl.when(half == 1)
            def _():
                pltpu.make_async_remote_copy(
                    resx.at[:, rows], backx.at[head], ret_sem, backx_sem,
                    device_id={"seq": r}, device_id_type=MESH_ID,
                ).start()

            return carry

        lax.fori_loop(0, GROUP, send_back, 0)

    pltpu.make_async_copy(back, back, back_sem).wait()

    @pl.when(half == 0)
    def _():
        pltpu.make_async_copy(backx, backx, backx_sem).wait()

    def sent_head(h, carry):
        @pl.when(worker_of(h, half) != me)
        def _():
            send_main(h).wait_send()

        @pl.when(half == 0)
        def _():
            send_cross(h).wait_send()

        return carry

    lax.fori_loop(0, H, sent_head, 0)

    @pl.when(is_worker)
    def _():
        def sent_back(i, carry):
            @pl.when(GROUP * half + i != me)
            def _():
                pltpu.make_async_remote_copy(
                    res.at[:, pl.ds(0, ROWS)], back.at[head], ret_sem, back_sem,
                    device_id={"seq": i}, device_id_type=MESH_ID,
                ).wait_send()

            @pl.when(half == 1)
            def _():
                pltpu.make_async_remote_copy(
                    resx.at[:, pl.ds(0, ROWS)], backx.at[head], ret_sem, backx_sem,
                    device_id={"seq": i}, device_id_type=MESH_ID,
                ).wait_send()

            return carry

        lax.fori_loop(0, GROUP, sent_back, 0)


def attention(head, half, recv, recvx, res, resx, col, row, kt, vt, sbuf, dpbuf, dkv):
    eye = (iota((HD, HD), 0) == iota((HD, HD), 1)).astype(jnp.bfloat16)
    eye_block = (iota((BLOCK, BLOCK), 0) == iota((BLOCK, BLOCK), 1)).astype(jnp.bfloat16)
    pick_a = (iota((HD, HD), 0) == 0).astype(jnp.bfloat16)
    pick_b = (iota((HD, HD), 0) == HD // 2).astype(jnp.bfloat16)
    key_refs = [(recv.at[K_A], recv.at[V_A]), (recv.at[K_B], recv.at[V_B]), (recvx.at[0], recvx.at[1])]
    for g, (k_ref, v_ref) in enumerate(key_refs):
        kt[g] = dot_nt(eye, k_ref[...]).astype(jnp.bfloat16)
        vt[g] = dot_nt(eye, v_ref[...]).astype(jnp.bfloat16)
    docs = recv[DOC]
    col[0] = dot_nn(docs, pick_a)
    col[1] = dot_nn(docs, pick_b)
    col[2] = jnp.where(half == 1, dot_nn(recvx[2], pick_a), -1.0)
    row[0] = dot_nt(one_hot_rows((8, HD), 0), docs)
    row[1] = dot_nt(one_hot_rows((8, HD), HD // 2), docs)

    lower = iota((BLOCK, BLOCK), 0) - iota((BLOCK, BLOCK), 1)
    b_is_later = jnp.where(head < FINEST, 1, 0)
    most = {(0, 0): 0, (1, 1): 0, (0, 1): -b_is_later, (1, 0): b_is_later - 1}
    started = set()
    for kind in (0, 1):
        for b in (0, 1):
            own = pl.ds(b * BLOCK, BLOCK)
            q = recv[Q_OF[kind], own]
            g = recv[D_OF[kind], own]
            q_docs = row[kind, 0:1, own]
            tiles = [(group, t) for group in (0, 1) for t in range(b + 1)]
            if kind == 0:
                tiles += [(2, 0), (2, 1)]
            top = None
            for n, (group, t) in enumerate(tiles):
                rows = pl.ds(t * BLOCK, BLOCK)
                s = dot_nt(key_refs[group][0][rows], q) * (SCORE_SCALE * LOG2_E)
                if kind == 0 and group == 0:
                    s = s + 1.0
                k_docs = col[group, rows]
                allowed = jnp.concatenate([k_docs, k_docs], 1) == q_docs
                if group < 2 and t == b:
                    allowed = allowed & (lower <= most[(kind, group)])
                s = jnp.where(allowed, s, MASKED)
                sbuf[n] = s
                tile_top = jnp.max(s, 0, keepdims=True)
                top = tile_top if top is None else jnp.maximum(top, tile_top)
            total = jnp.zeros((1, BLOCK), jnp.float32)
            drop = jnp.zeros((1, BLOCK), jnp.float32)
            for n, (group, t) in enumerate(tiles):
                rows = pl.ds(t * BLOCK, BLOCK)
                e = jnp.exp2(sbuf[n] - top)
                dp = dot_nt(key_refs[group][1][rows], g)
                total = total + jnp.sum(e, 0, keepdims=True)
                drop = drop + jnp.sum(e * dp, 0, keepdims=True)
                sbuf[n] = e
                dpbuf[n] = dp
            inverse = 1.0 / total
            drop = drop * inverse
            out_t = jnp.zeros((HD, BLOCK), jnp.float32)
            dq_t = jnp.zeros((HD, BLOCK), jnp.float32)
            for n, (group, t) in enumerate(tiles):
                rows = pl.ds(t * BLOCK, BLOCK)
                w = sbuf[n] * inverse
                ds = (w * (dpbuf[n] - drop)).astype(jnp.bfloat16)
                w = w.astype(jnp.bfloat16)
                out_t = out_t + dot_nn(vt[group, :, rows], w)
                dq_t = dq_t + dot_nn(kt[group, :, rows], ds)
                dk = dot_nn(ds, q)
                dv = dot_nn(w, g)
                if (group, t) in started:
                    dk = dk + dkv[0, group, rows]
                    dv = dv + dkv[1, group, rows]
                started.add((group, t))
                dkv[0, group, rows] = dk
                dkv[1, group, rows] = dv
            res[kind, own] = dot_nt(eye_block, out_t.astype(jnp.bfloat16)).astype(jnp.bfloat16)
            dq = (dq_t * SCORE_SCALE).astype(jnp.bfloat16)
            res[2 + kind, own] = dot_nt(eye_block, dq).astype(jnp.bfloat16)
    for kind in (0, 1):
        res[4 + kind] = (dkv[0, kind] * SCORE_SCALE).astype(jnp.bfloat16)
        res[6 + kind] = dkv[1, kind].astype(jnp.bfloat16)
    resx[0] = (dkv[0, 2] * SCORE_SCALE).astype(jnp.bfloat16)
    resx[1] = dkv[1, 2].astype(jnp.bfloat16)


def place_kernel(back, backx, o_ref, dq_ref, dk_ref, dv_ref):
    first = lax.axis_index("seq") < GROUP
    for h in range(H):
        shape = (TOKENS, 2 * ROWS)
        rank = iota(shape, 1)
        kind = (h + FINEST * (rank >> 4)) & (CLASSES - 1)
        spread = (iota(shape, 0) == CLASSES * (rank & (ROWS - 1)) + kind).astype(jnp.bfloat16)
        lanes = pl.ds(h * HD, HD)
        for i, ref in enumerate((o_ref, dq_ref, dk_ref, dv_ref)):
            rows = back[h, 2 * i : 2 * i + 2].reshape(2 * ROWS, HD)
            if i >= 2:
                extra = jnp.where(first, backx[h, i - 2].astype(jnp.float32), 0.0)
                summed = (back[h, 2 * i].astype(jnp.float32) + extra).astype(jnp.bfloat16)
                rows = jnp.concatenate([summed, back[h, 2 * i + 1]], 0)
            ref[:, lanes] = dot_nn(spread, rows).astype(jnp.bfloat16)


def per_device(queries, keys, values, cotangent, doc_ids):
    any_space = pl.BlockSpec(memory_space=pl.ANY)
    vmem = pl.BlockSpec(memory_space=pltpu.VMEM)
    bf16, f32 = jnp.bfloat16, jnp.float32
    dma = pltpu.SemaphoreType.DMA
    back, backx = pl.pallas_call(
        exchange_kernel,
        out_shape=(
            jax.ShapeDtypeStruct((H, 8, ROWS, HD), bf16),
            jax.ShapeDtypeStruct((H, 2, ROWS, HD), bf16),
        ),
        in_specs=[any_space] * 4 + [vmem],
        out_specs=(any_space, any_space),
        scratch_shapes=[
            pltpu.VMEM((4, TOKENS, H * HD), bf16),
            pltpu.VMEM((H, 9, ROWS, HD), bf16),
            pltpu.VMEM((9, SEG_ROWS, HD), bf16),
            pltpu.VMEM((3, SEG_ROWS, HD), bf16),
            pltpu.VMEM((8, SEG_ROWS, HD), bf16),
            pltpu.VMEM((2, SEG_ROWS, HD), bf16),
            pltpu.VMEM((3, SEG_ROWS, HD), f32),
            pltpu.VMEM((2, 8, SEG_ROWS), f32),
            pltpu.VMEM((3, HD, SEG_ROWS), bf16),
            pltpu.VMEM((3, HD, SEG_ROWS), bf16),
            pltpu.VMEM((6, BLOCK, BLOCK), f32),
            pltpu.VMEM((6, BLOCK, BLOCK), f32),
            pltpu.VMEM((2, 3, SEG_ROWS, HD), f32),
            dma((4,)),
            dma,
            dma,
            dma,
            dma,
            dma,
            dma,
        ],
        compiler_params=pltpu.CompilerParams(
            collective_id=0, has_side_effects=True, vmem_limit_bytes=48 * 2**20
        ),
        name="exchange",
    )(queries, keys, values, cotangent, doc_ids.reshape(1, TOKENS))
    full = jax.ShapeDtypeStruct((TOKENS, H * HD), bf16)
    return tuple(
        pl.pallas_call(
            place_kernel,
            out_shape=(full,) * 4,
            in_specs=[vmem, vmem],
            out_specs=(vmem,) * 4,
            name="place",
        )(back, backx)
    )


def solution(mesh):
    spec = P(("dp", "seq"), None)
    return jax.shard_map(
        per_device,
        mesh=mesh,
        in_specs=(spec, spec, spec, spec, P(("dp", "seq"))),
        out_specs=(spec,) * 4,
        check_vma=False,
    )
```

time: 905 us -> 49.5 us (0.05)
  waiting for transfers between devices: 408 us -> 0 us
  starting transfers between devices: 339 us -> 0 us
  local copies, waits for them, and re-layouts: 99.3 us -> 5.75 us
  Pallas kernels: 0 us -> 42.4 us
  matrix products: 24.4 us -> 0 us
  other arithmetic: 21.7 us -> 0 us
    ppermute x88 -> x0, waiting for transfers between devices: 408 us -> none  [from_partner(): lax.ppermute(shard, axis, [(i, i ^ 1 << stride) for i in range(lax.axis_s...]
    ppermute x88 -> x0, starting transfers between devices: 339 us -> none  [from_partner(): lax.ppermute(shard, axis, [(i, i ^ 1 << stride) for i in range(lax.axis_s...]
    pallas_call x0 -> x2, Pallas kernels: none -> 42.4 us  [the longest x1 40.1 us: per_device(): pl.pallas_call(exchange_kernel, out_shape=(jax.ShapeDtypeStruct((H, 8, RO...]
    unnamed x187 -> x14, local copies, waits for them, and re-layouts: 32.3 us -> 5.75 us
    concatenate x41 -> x0, local copies, waits for them, and re-layouts: 26.3 us -> none  [the longest x36 25.9 us: join_pair(): jnp.concatenate([own_part, their_part], 0)]
    dot_general x12 -> x0, matrix products: 24.4 us -> none  [the longest x4 6.63 us: level_scores(): jnp.einsum('ihd,jhd->hij', query_sel, key_sel, preferred_element_type=jnp...]
    scatter x21 -> x0, local copies, waits for them, and re-layouts: 22.5 us -> none  [place_rows(): empty.at[:, np.arange(heads) % dilation_step, np.arange(heads)].set(array)]
    gather x14 -> x0, local copies, waits for them, and re-layouts: 10.4 us -> none  [dilate(): return shaped[:, np.arange(heads) % dilation_step, np.arange(heads)]]
  transfers between devices with their start and end apart: 88 -> 0, of which waited for: 14 -> 0; matrix products, arithmetic and copies ran while one was open for 15% -> 0% of each run, Pallas kernels for 0% -> 0%
where the time goes in v1:
time: 49.5 us; the launch traced here: 48.8 us
  Pallas kernels  42.4 us (86%)
  local copies, waits for them, and re-layouts  5.75 us (12%)
  between operations  0.66 us (1%)
    pallas_call x1, Pallas kernels, per_device(): pl.pallas_call(exchange_kernel, out_shape=(jax.ShapeDtypeStruct((H, 8, RO...  40.1 us
    unnamed x14, local copies, waits for them, and re-layouts  5.75 us
    pallas_call x1, Pallas kernels, per_device(): pl.pallas_call(place_kernel, out_shape=(full,) * 4, in_specs=[vmem, vmem]...  2.35 us

profile of v1, /device:TPU:1, one launch (start us, length us, event | category | flops | bytes accessed | tf_op | source)
XLA Modules:
  0.0 48.8 jit_solution(12248054355003156346)
XLA Ops:
  0.6 0.0 copy-start.6
  0.6 0.6 %copy-done.6 = s32[128]{0:T(128)S(1)} copy-done((s32[128]{0:T(128)S(1)}, s32[128]{0:T(128)}, u32[]{:S(2)}) %copy-start.6) | copy-done | bytes 536
  1.3 0.0 copy-start.1
  1.3 0.9 %copy-done.1 = bf16[128,1024]{1,0:T(8,128)(2,1)S(1)} copy-done((bf16[128,1024]{1,0:T(8,128)(2,1)S(1)}, bf16[128,1024]{1,0:T(8,128)(2,1)}, u32[]{:S(2)}) %copy-start.1) | copy-done | bytes 262168
  2.2 0.0 copy-start.2
  2.2 0.9 %copy-done.2 = bf16[128,1024]{1,0:T(8,128)(2,1)S(1)} copy-done((bf16[128,1024]{1,0:T(8,128)(2,1)S(1)}, bf16[128,1024]{1,0:T(8,128)(2,1)}, u32[]{:S(2)}) %copy-start.2) | copy-done | bytes 262168
  3.2 0.0 copy-start.3
  3.2 0.9 %copy-done.3 = bf16[128,1024]{1,0:T(8,128)(2,1)S(1)} copy-done((bf16[128,1024]{1,0:T(8,128)(2,1)S(1)}, bf16[128,1024]{1,0:T(8,128)(2,1)}, u32[]{:S(2)}) %copy-start.3) | copy-done | bytes 262168
  4.1 0.0 copy-start.4
  4.1 0.9 %copy-done.4 = bf16[128,1024]{1,0:T(8,128)(2,1)S(1)} copy-done((bf16[128,1024]{1,0:T(8,128)(2,1)S(1)}, bf16[128,1024]{1,0:T(8,128)(2,1)}, u32[]{:S(2)}) %copy-start.4) | copy-done | bytes 262168
  5.1 40.1 %exchange.1 = (bf16[8,8,16,128]{3,2,1,0:T(8,128)(2,1)S(1)}, bf16[8,2,16,128]{3,2,1,0:T(8,128)(2,1)S(1)}) custom-call(bf16[128,1024]{1,0:T(8,128)(2,1)S(1)} %copy-done.1, bf16[128,1024]{1,0:T(8,128)(2,1)S(1)} %copy-done.2, bf16[128,1024]{1,0:T(8,128)(2,1)S(1)} %copy-done.3, bf16[128,1024]{1,0:T(8,128)(2,1)S(1)} %copy-done.4, s32[1,128]{1,0:T(1,128)S(1)} %bitcast.1), custom_call_target="tpu_custom_call" | custom-call | tf_op jit(solution)/shard_map/exchange/pallas_call | solution.py:328
  45.2 0.0 copy-start
  45.2 0.7 %copy-done = bf16[8,8,16,128]{3,2,1,0:T(8,128)(2,1)} copy-done((bf16[8,8,16,128]{3,2,1,0:T(8,128)(2,1)}, bf16[8,8,16,128]{3,2,1,0:T(8,128)(2,1)S(1)}, u32[]{:S(2)}) %copy-start) | copy-done | bytes 262168
  45.9 0.0 copy-start.5
  45.9 0.6 %copy-done.5 = bf16[8,2,16,128]{3,2,1,0:T(8,128)(2,1)} copy-done((bf16[8,2,16,128]{3,2,1,0:T(8,128)(2,1)}, bf16[8,2,16,128]{3,2,1,0:T(8,128)(2,1)S(1)}, u32[]{:S(2)}) %copy-start.5) | copy-done | bytes 65560
  46.5 2.4 %place.1 = (bf16[128,1024]{1,0:T(8,128)(2,1)}, bf16[128,1024]{1,0:T(8,128)(2,1)}, bf16[128,1024]{1,0:T(8,128)(2,1)}, bf16[128,1024]{1,0:T(8,128)(2,1)}) custom-call(bf16[8,8,16,128]{3,2,1,0:T(8,128)(2,1)} %copy-done, bf16[8,2,16,128]{3,2,1,0:T(8,128)(2,1)} %copy-done.5), custom_call_target="tpu_custom_call" | custom-call | tf_op jit(solution)/shard_map/place/pallas_call | solution.py:365
Async XLA Ops:
  0.6 0.7 %copy-start.6 = (s32[128]{0:T(128)S(1)}, s32[128]{0:T(128)}, u32[]{:S(2)}) copy-start(s32[128]{0:T(128)} %param.9) | copy-start | bytes 1540
  1.3 0.9 %copy-start.1 = (bf16[128,1024]{1,0:T(8,128)(2,1)S(1)}, bf16[128,1024]{1,0:T(8,128)(2,1)}, u32[]{:S(2)}) copy-start(bf16[128,1024]{1,0:T(8,128)(2,1)} %q_hbm.1) | copy-start | bytes 786436
  2.2 0.9 %copy-start.2 = (bf16[128,1024]{1,0:T(8,128)(2,1)S(1)}, bf16[128,1024]{1,0:T(8,128)(2,1)}, u32[]{:S(2)}) copy-start(bf16[128,1024]{1,0:T(8,128)(2,1)} %k_hbm.1) | copy-start | bytes 786436
  3.2 0.9 %copy-start.3 = (bf16[128,1024]{1,0:T(8,128)(2,1)S(1)}, bf16[128,1024]{1,0:T(8,128)(2,1)}, u32[]{:S(2)}) copy-start(bf16[128,1024]{1,0:T(8,128)(2,1)} %v_hbm.1) | copy-start | bytes 786436
  4.1 0.9 %copy-start.4 = (bf16[128,1024]{1,0:T(8,128)(2,1)S(1)}, bf16[128,1024]{1,0:T(8,128)(2,1)}, u32[]{:S(2)}) copy-start(bf16[128,1024]{1,0:T(8,128)(2,1)} %g_hbm.1) | copy-start | bytes 786436
  45.2 0.7 %copy-start = (bf16[8,8,16,128]{3,2,1,0:T(8,128)(2,1)}, bf16[8,8,16,128]{3,2,1,0:T(8,128)(2,1)S(1)}, u32[]{:S(2)}) copy-start(bf16[8,8,16,128]{3,2,1,0:T(8,128)(2,1)S(1)} %get-tuple-element.6.back) | copy-start | bytes 786436
  45.9 0.6 %copy-start.5 = (bf16[8,2,16,128]{3,2,1,0:T(8,128)(2,1)}, bf16[8,2,16,128]{3,2,1,0:T(8,128)(2,1)S(1)}, u32[]{:S(2)}) copy-start(bf16[8,2,16,128]{3,2,1,0:T(8,128)(2,1)S(1)} %get-tuple-element.7.backx) | copy-start | bytes 196612

commit v2 on v1

v2 whole, which is shorter than its diff:
```python
import jax
import jax.numpy as jnp
from jax import lax
from jax.experimental import pallas as pl
from jax.experimental.pallas import tpu as pltpu
from jax.sharding import PartitionSpec as P

H = 8
HD = 128
SEQ_DEVICES = 64
GROUP = 32
TOKENS = 128
ROWS = 16
SEG_ROWS = GROUP * ROWS
BLOCK = 256
CLASSES = 8
FINEST = 4
SCORE_SCALE = HD**-0.5
LOG2_E = 1.4426950408889634
MASKED = -1e30
MESH_ID = pl.DeviceIdType.MESH

MESSAGE = 8 * ROWS + 8
CROSS_AT = 6 * ROWS
CROSS = MESSAGE - CROSS_AT

Q_OF, K_OF, V_OF, D_OF = (0, 1), (6, 4), (7, 5), (2, 3)


def dot_nn(a, b):
    return jnp.dot(a, b, preferred_element_type=jnp.float32)


def dot_nt(a, b):
    return lax.dot_general(a, b, (((1,), (1,)), ((), ())), preferred_element_type=jnp.float32)


def iota(shape, dim):
    return lax.broadcasted_iota(jnp.int32, shape, dim)


def selector(head):
    shape = (2 * ROWS, TOKENS)
    row = iota(shape, 0)
    kind = (head + FINEST * (row >> 4)) & (CLASSES - 1)
    return iota(shape, 1) == CLASSES * (row & (ROWS - 1)) + kind


def worker_of(head, half):
    return GROUP * half + 8 + 2 * head


def exchange_kernel(
    q_hbm, k_hbm, v_hbm, g_hbm, doc_ref, back, backx,
    xin, snd, recv, recvx, res, resx, kt, vt, s0, dp0, e_own, dp_own, stat, ot0, dqt0, dkv,
    in_sem, send_sem, recv_sem, recvx_sem, ret_sem, back_sem, backx_sem,
):
    me = lax.axis_index("seq")
    half = me // GROUP
    rank = lax.rem(me, GROUP)
    is_worker = (rank >= 8) & (rank < 24) & (lax.rem(rank, 2) == 0)
    head = (rank - 8) // 2

    loads = [
        pltpu.make_async_copy(ref, xin.at[i], in_sem.at[i])
        for i, ref in enumerate((q_hbm, k_hbm, v_hbm, g_hbm))
    ]
    for load in loads:
        load.start()

    barrier = pltpu.get_barrier_semaphore()

    def greet(device):
        @pl.when(device != me)
        def _():
            pl.semaphore_signal(barrier, inc=1, device_id={"seq": device}, device_id_type=MESH_ID)

    @pl.when(half == 0)
    def _():
        lax.fori_loop(0, H, lambda i, c: (greet(worker_of(i, 0)), c)[1], 0)

    lax.fori_loop(0, H, lambda i, c: (greet(worker_of(i, 1)), c)[1], 0)

    @pl.when(is_worker)
    def _():
        lax.fori_loop(0, GROUP * (1 + half), lambda i, c: (greet(i), c)[1], 0)

    docs = jnp.broadcast_to(doc_ref[...].astype(jnp.float32), (8, TOKENS)).astype(jnp.bfloat16)
    for h in range(H):
        snd[h, 8 * ROWS : MESSAGE] = docs
    one_hots = [selector(h).astype(jnp.bfloat16) for h in range(H)]
    for i, slots in enumerate((Q_OF, K_OF, V_OF, D_OF)):
        loads[i].wait()
        for h in range(H):
            rows = dot_nn(one_hots[h], xin[i, :, h * HD : (h + 1) * HD]).astype(jnp.bfloat16)
            for kind, slot in enumerate(slots):
                snd[h, slot * ROWS : (slot + 1) * ROWS] = rows[kind * ROWS : (kind + 1) * ROWS]

    own_sources = jnp.where(is_worker, GROUP * (1 + half) - 1, 0)
    own_workers = jnp.where(half == 0, 2 * H, H) - jnp.where(is_worker, 1, 0)
    pl.semaphore_wait(barrier, own_sources + own_workers)


    def send_main(h):
        return pltpu.make_async_remote_copy(
            snd.at[h], recv.at[rank], send_sem, recv_sem,
            device_id={"seq": worker_of(h, half)}, device_id_type=MESH_ID,
        )

    def send_cross(h):
        return pltpu.make_async_remote_copy(
            snd.at[h, pl.ds(CROSS_AT, CROSS)], recvx.at[rank], send_sem, recvx_sem,
            device_id={"seq": worker_of(h, 1)}, device_id_type=MESH_ID,
        )

    def send_head(i, carry):
        h = lax.rem(i + me, H)
        target = worker_of(h, half)

        @pl.when(target != me)
        def _():
            send_main(h).start()

        @pl.when(target == me)
        def _():
            pltpu.make_async_copy(snd.at[h], recv.at[rank], recv_sem).start()

        return carry

    def send_cross_head(i, carry):
        send_cross(lax.rem(i + me, H)).start()
        return carry

    @pl.when(half == 0)
    def _():
        lax.fori_loop(0, H, send_cross_head, 0)

    lax.fori_loop(0, H, send_head, 0)

    @pl.when(is_worker)
    def _():
        pltpu.make_async_copy(recv, recv, recv_sem).wait()

        @pl.when(half == 1)
        def _():
            pltpu.make_async_copy(recvx, recvx, recvx_sem).wait()

        def send_cross_back(i, carry):
            r = lax.rem(i + rank, GROUP)
            pltpu.make_async_remote_copy(
                resx.at[r], backx.at[head], ret_sem, backx_sem,
                device_id={"seq": r}, device_id_type=MESH_ID,
            ).start()
            return carry

        def send_back(block):
            def one(i, carry):
                r = block * 8 + lax.rem(i + rank, 8)
                target = GROUP * half + r

                @pl.when(target != me)
                def _():
                    pltpu.make_async_remote_copy(
                        res.at[r], back.at[head], ret_sem, back_sem,
                        device_id={"seq": target}, device_id_type=MESH_ID,
                    ).start()

                @pl.when(target == me)
                def _():
                    pltpu.make_async_copy(res.at[r], back.at[head], back_sem).start()

                return carry

            lax.fori_loop(0, 8, one, 0)

        def send_crosses():
            lax.fori_loop(0, GROUP, send_cross_back, 0)

        attention(
            head, half, recv, recvx, res, resx, kt, vt, s0, dp0, e_own, dp_own, stat, ot0, dqt0, dkv,
            send_crosses, send_back,
        )

    pltpu.make_async_copy(back, back, back_sem).wait()

    @pl.when(half == 0)
    def _():
        pltpu.make_async_copy(backx, backx, backx_sem).wait()

    def sent_head(h, carry):
        @pl.when(worker_of(h, half) != me)
        def _():
            send_main(h).wait_send()

        @pl.when(half == 0)
        def _():
            send_cross(h).wait_send()

        return carry

    lax.fori_loop(0, H, sent_head, 0)

    @pl.when(is_worker)
    def _():
        def sent_back(i, carry):
            @pl.when(GROUP * half + i != me)
            def _():
                pltpu.make_async_remote_copy(
                    res.at[i], back.at[head], ret_sem, back_sem,
                    device_id={"seq": i}, device_id_type=MESH_ID,
                ).wait_send()

            @pl.when(half == 1)
            def _():
                pltpu.make_async_remote_copy(
                    resx.at[i], backx.at[head], ret_sem, backx_sem,
                    device_id={"seq": i}, device_id_type=MESH_ID,
                ).wait_send()

            return carry

        lax.fori_loop(0, GROUP, sent_back, 0)


def tile_rows(ref, tile):
    return ref[:, tile * ROWS : (tile + 1) * ROWS].reshape(SEG_ROWS, HD)


def class_docs(ref, at, kind):
    eight = ref[:, at : at + 8].astype(jnp.float32)
    spread = jnp.concatenate([eight, eight], 1).reshape(SEG_ROWS, HD)
    shape = (SEG_ROWS, HD)
    own = iota(shape, 1) == CLASSES * (iota(shape, 0) & (ROWS - 1)) + kind
    picked = jnp.where(own, spread, 0.0).astype(jnp.bfloat16)
    ones = jnp.ones((HD, HD), jnp.bfloat16)
    return dot_nn(picked, ones), dot_nt(ones[:8], picked)


def attention(
    head, half, recv, recvx, res, resx, kt, vt, s0, dp0, e_own, dp_own, stat, ot0, dqt0, dkv,
    send_crosses, send_back,
):
    bf16, f32 = jnp.bfloat16, jnp.float32
    scale = SCORE_SCALE * LOG2_E
    eye = (iota((HD, HD), 0) == iota((HD, HD), 1)).astype(bf16)
    eye_block = (iota((BLOCK, BLOCK), 0) == iota((BLOCK, BLOCK), 1)).astype(bf16)
    q_all = [tile_rows(recv, t) for t in Q_OF]
    k_all = [tile_rows(recv, t) for t in K_OF]
    v_all = [tile_rows(recv, t) for t in V_OF]
    g_all = [tile_rows(recv, t) for t in D_OF]
    for kind in (0, 1):
        kt[kind] = dot_nt(eye, k_all[kind]).astype(bf16)
        vt[kind] = dot_nt(eye, v_all[kind]).astype(bf16)
    docs = [class_docs(recv, 8 * ROWS, (head + FINEST * kind) & (CLASSES - 1)) for kind in (0, 1)]
    cols = [d[0] for d in docs]
    q_docs = [d[1][0:1] for d in docs]

    stat[0] = jnp.full((8, SEG_ROWS), MASKED, f32)
    stat[1] = jnp.zeros((8, SEG_ROWS), f32)
    stat[2] = jnp.zeros((8, SEG_ROWS), f32)
    ot0[...] = jnp.zeros_like(ot0)
    dqt0[...] = jnp.zeros_like(dqt0)

    @pl.when(half == 1)
    def _():
        col0, _ = class_docs(recvx, 2 * ROWS, head)
        k0 = tile_rows(recvx, 0)
        kt[2] = dot_nt(eye, k0).astype(bf16)
        vt[2] = dot_nt(eye, tile_rows(recvx, 1)).astype(bf16)
        for c in range(0, SEG_ROWS, BLOCK):
            at = pl.ds(c, BLOCK)
            query = q_all[0][c : c + BLOCK]
            top = None
            for r in range(0, SEG_ROWS, BLOCK):
                doc = col0[r : r + BLOCK]
                s = dot_nt(k0[r : r + BLOCK], query) * scale
                allowed = jnp.concatenate([doc, doc], 1) == q_docs[0][:, c : c + BLOCK]
                s = jnp.where(allowed, s, MASKED)
                s0[pl.ds(r, BLOCK), at] = s
                t = jnp.max(s, 0, keepdims=True)
                top = t if top is None else jnp.maximum(top, t)
            stat[0, 0:1, at] = top

    lower = iota((HD, BLOCK), 0) - (iota((HD, BLOCK), 1) & (HD - 1))
    is_a = iota((HD, BLOCK), 1) < HD
    b_is_later = jnp.where(head < FINEST, 1, 0)
    in_order = [
        lower <= jnp.where(is_a, 0, b_is_later - 1),
        lower <= jnp.where(is_a, -b_is_later, 0),
    ]
    bonus = jnp.where(iota((1, BLOCK), 1) < HD, 1.0, 0.0)
    both = lambda pair, i: jnp.concatenate([pair[0][i * HD : (i + 1) * HD], pair[1][i * HD : (i + 1) * HD]], 0)
    lanes = lambda pair, i: jnp.concatenate([pair[0][:, i * HD : (i + 1) * HD], pair[1][:, i * HD : (i + 1) * HD]], 1)
    blocks = SEG_ROWS // HD
    qs = [both(q_all, i) for i in range(blocks)]
    gs = [both(g_all, i) for i in range(blocks)]
    totals, drops = [], []
    for i in range(blocks):
        query_docs = lanes(q_docs, i)
        at = pl.ds(i * HD, HD)
        top = jnp.concatenate([stat[0, 0:1, at], jnp.full((1, HD), MASKED, f32)], 1)
        for kind in (0, 1):
            for t in range(i + 1):
                rows = slice(t * HD, (t + 1) * HD)
                s = dot_nt(k_all[kind][rows], qs[i]) * scale
                if kind == 0:
                    s = s + bonus
                doc = cols[kind][rows]
                allowed = jnp.concatenate([doc, doc], 1) == query_docs
                if t == i:
                    allowed = allowed & in_order[kind]
                s = jnp.where(allowed, s, MASKED)
                e_own[i, kind, rows] = s
                top = jnp.maximum(top, jnp.max(s, 0, keepdims=True))
        stat[0, 0:1, at] = top[:, :HD]
        total = jnp.zeros((1, BLOCK), f32)
        drop = jnp.zeros((1, BLOCK), f32)
        for kind in (0, 1):
            for t in range(i + 1):
                rows = slice(t * HD, (t + 1) * HD)
                e = jnp.exp2(e_own[i, kind, rows] - top)
                dp = dot_nt(v_all[kind][rows], gs[i])
                total = total + jnp.sum(e, 0, keepdims=True)
                drop = drop + jnp.sum(e * dp, 0, keepdims=True)
                e_own[i, kind, rows] = e
                dp_own[i, kind, rows] = dp
        totals.append(total)
        drops.append(drop)
    for i in range(blocks):
        at = pl.ds(i * HD, HD)
        stat[1, 0:1, at] = totals[i][:, :HD]
        stat[2, 0:1, at] = drops[i][:, :HD]

    @pl.when(half == 1)
    def _():
        v0 = tile_rows(recvx, 1)
        dk, dv = None, None
        for c in range(0, SEG_ROWS, BLOCK):
            at = pl.ds(c, BLOCK)
            query, grad = q_all[0][c : c + BLOCK], g_all[0][c : c + BLOCK]
            top = stat[0, 0:1, at]
            total, drop = stat[1, 0:1, at], stat[2, 0:1, at]
            for r in range(0, SEG_ROWS, BLOCK):
                rows = pl.ds(r, BLOCK)
                e = jnp.exp2(s0[rows, at] - top)
                dp = dot_nt(v0[r : r + BLOCK], grad)
                total = total + jnp.sum(e, 0, keepdims=True)
                drop = drop + jnp.sum(e * dp, 0, keepdims=True)
                s0[rows, at] = e
                dp0[rows, at] = dp
            stat[1, 0:1, at] = total
            stat[2, 0:1, at] = drop
            inverse = 1.0 / total
            drop = drop * inverse
            for r in range(0, SEG_ROWS, BLOCK):
                rows = pl.ds(r, BLOCK)
                w = s0[rows, at] * inverse
                ds = (w * (dp0[rows, at] - drop)).astype(bf16)
                w = w.astype(bf16)
                ot0[:, at] += dot_nn(vt[2, :, rows], w)
                dqt0[:, at] += dot_nn(kt[2, :, rows], ds)
                dk, dv = dot_nn(ds, query), dot_nn(w, grad)
                if c:
                    dk = dk + dkv[0, 2, rows]
                    dv = dv + dkv[1, 2, rows]
                dkv[0, 2, rows] = dk
                dkv[1, 2, rows] = dv
        resx[:, :ROWS] = (dkv[0, 2] * SCORE_SCALE).astype(bf16).reshape(GROUP, ROWS, HD)
        resx[:, ROWS:] = dkv[1, 2].astype(bf16).reshape(GROUP, ROWS, HD)
        send_crosses()

    started = False
    for i in reversed(range(blocks)):
        at = pl.ds(i * HD, HD)
        n = (i + 1) * HD
        total = jnp.concatenate([stat[1, 0:1, at], totals[i][:, HD:]], 1)
        drop = jnp.concatenate([stat[2, 0:1, at], drops[i][:, HD:]], 1)
        inverse = 1.0 / total
        drop = drop * inverse
        out_t = jnp.concatenate([ot0[:, at], jnp.zeros((HD, HD), f32)], 1)
        dq_t = jnp.concatenate([dqt0[:, at], jnp.zeros((HD, HD), f32)], 1)
        for kind in (0, 1):
            w = e_own[i, kind, :n] * inverse
            ds = (w * (dp_own[i, kind, :n] - drop)).astype(bf16)
            w = w.astype(bf16)
            out_t = out_t + dot_nn(vt[kind, :, :n], w)
            dq_t = dq_t + dot_nn(kt[kind, :, :n], ds)
            dk, dv = dot_nn(ds, qs[i]), dot_nn(w, gs[i])
            if started:
                dk = dk + dkv[0, kind, :n]
                dv = dv + dkv[1, kind, :n]
            dkv[0, kind, :n] = dk
            dkv[1, kind, :n] = dv
        started = True
        out = dot_nt(eye_block, out_t.astype(bf16)).astype(bf16)
        dq = dot_nt(eye_block, (dq_t * SCORE_SCALE).astype(bf16)).astype(bf16)
        owners = slice(8 * i, 8 * i + 8)
        for kind in (0, 1):
            tiles = (
                out[kind * HD : (kind + 1) * HD],
                dq[kind * HD : (kind + 1) * HD],
                (dkv[0, kind, at] * SCORE_SCALE).astype(bf16),
                dkv[1, kind, at].astype(bf16),
            )
            for t, tile in enumerate(tiles):
                slot = (2 * t + kind) * ROWS
                res[owners, slot : slot + ROWS] = tile.reshape(8, ROWS, HD)
        send_back(i)


def place_kernel(back, backx, o_ref, dq_ref, dk_ref, dv_ref):
    first = lax.axis_index("seq") < GROUP
    for h in range(H):
        shape = (TOKENS, 2 * ROWS)
        rank = iota(shape, 1)
        kind = (h + FINEST * (rank >> 4)) & (CLASSES - 1)
        spread = (iota(shape, 0) == CLASSES * (rank & (ROWS - 1)) + kind).astype(jnp.bfloat16)
        lanes = pl.ds(h * HD, HD)
        for i, ref in enumerate((o_ref, dq_ref, dk_ref, dv_ref)):
            rows = back[h, 2 * i * ROWS : (2 * i + 2) * ROWS]
            if i >= 2:
                extra = jnp.where(first, backx[h, (i - 2) * ROWS : (i - 1) * ROWS].astype(jnp.float32), 0.0)
                summed = (rows[:ROWS].astype(jnp.float32) + extra).astype(jnp.bfloat16)
                rows = jnp.concatenate([summed, rows[ROWS:]], 0)
            ref[:, lanes] = dot_nn(spread, rows).astype(jnp.bfloat16)


def per_device(queries, keys, values, cotangent, doc_ids):
    any_space = pl.BlockSpec(memory_space=pl.ANY)
    vmem = pl.BlockSpec(memory_space=pltpu.VMEM)
    bf16, f32 = jnp.bfloat16, jnp.float32
    dma = pltpu.SemaphoreType.DMA
    back, backx = pl.pallas_call(
        exchange_kernel,
        out_shape=(
            jax.ShapeDtypeStruct((H, 8 * ROWS, HD), bf16),
            jax.ShapeDtypeStruct((H, 2 * ROWS, HD), bf16),
        ),
        in_specs=[any_space] * 4 + [vmem],
        out_specs=(any_space, any_space),
        scratch_shapes=[
            pltpu.VMEM((4, TOKENS, H * HD), bf16),
            pltpu.VMEM((H, MESSAGE, HD), bf16),
            pltpu.VMEM((GROUP, MESSAGE, HD), bf16),
            pltpu.VMEM((GROUP, CROSS, HD), bf16),
            pltpu.VMEM((GROUP, 8 * ROWS, HD), bf16),
            pltpu.VMEM((GROUP, 2 * ROWS, HD), bf16),
            pltpu.VMEM((3, HD, SEG_ROWS), bf16),
            pltpu.VMEM((3, HD, SEG_ROWS), bf16),
            pltpu.VMEM((SEG_ROWS, SEG_ROWS), f32),
            pltpu.VMEM((SEG_ROWS, SEG_ROWS), f32),
            pltpu.VMEM((SEG_ROWS // HD, 2, SEG_ROWS, BLOCK), f32),
            pltpu.VMEM((SEG_ROWS // HD, 2, SEG_ROWS, BLOCK), f32),
            pltpu.VMEM((3, 8, SEG_ROWS), f32),
            pltpu.VMEM((HD, SEG_ROWS), f32),
            pltpu.VMEM((HD, SEG_ROWS), f32),
            pltpu.VMEM((2, 3, SEG_ROWS, HD), f32),
            dma((4,)),
            dma,
            dma,
            dma,
            dma,
            dma,
            dma,
        ],
        compiler_params=pltpu.CompilerParams(
            collective_id=0, has_side_effects=True, vmem_limit_bytes=62 * 2**20
        ),
        name="exchange",
    )(queries, keys, values, cotangent, doc_ids.reshape(1, TOKENS))
    full = jax.ShapeDtypeStruct((TOKENS, H * HD), bf16)
    return tuple(
        pl.pallas_call(
            place_kernel,
            out_shape=(full,) * 4,
            in_specs=[vmem, vmem],
            out_specs=(vmem,) * 4,
            name="place",
        )(back, backx)
    )


def solution(mesh):
    spec = P(("dp", "seq"), None)
    return jax.shard_map(
        per_device,
        mesh=mesh,
        in_specs=(spec, spec, spec, spec, P(("dp", "seq"))),
        out_specs=(spec,) * 4,
        check_vma=False,
    )
```

time: 49.5 us -> 38 us (0.77)
  local copies, waits for them, and re-layouts: 5.75 us -> 0 us
  Pallas kernels: 42.4 us -> 36.8 us
    unnamed x14 -> x0, local copies, waits for them, and re-layouts: 5.75 us -> none
    pallas_call x1, Pallas kernels: 40.1 us -> 34.5 us  [per_device(): pl.pallas_call(exchange_kernel, out_shape=(jax.ShapeDtypeStruct((H, 8 * R...]
where the time goes in v2:
time: 38 us; the launch traced here: 37.5 us
  Pallas kernels  36.8 us (97%)
  between operations  0.64 us (2%)
    pallas_call x1, Pallas kernels, per_device(): pl.pallas_call(exchange_kernel, out_shape=(jax.ShapeDtypeStruct((H, 8 * R...  34.5 us
    pallas_call x1, Pallas kernels, per_device(): pl.pallas_call(place_kernel, out_shape=(full,) * 4, in_specs=[vmem, vmem]...  2.35 us

profile of v2, /device:TPU:1, one launch (start us, length us, event | category | flops | bytes accessed | tf_op | source)
XLA Modules:
  0.0 37.5 jit_solution(3539629138638046528)
XLA Ops:
  0.6 34.5 %exchange.1 = (bf16[8,128,128]{2,1,0:T(8,128)(2,1)}, bf16[8,32,128]{2,1,0:T(8,128)(2,1)}) custom-call(bf16[128,1024]{1,0:T(8,128)(2,1)} %q_hbm.1, bf16[128,1024]{1,0:T(8,128)(2,1)} %k_hbm.1, bf16[128,1024]{1,0:T(8,128)(2,1)} %v_hbm.1, bf16[128,1024]{1,0:T(8,128)(2,1)} %g_hbm.1, s32[1,128]{1,0:T(1,128)} %bitcast.1), custom_call_target="tpu_custom_call" | custom-call | tf_op jit(solution)/shard_map/exchange/pallas_call | solution.py:433
  35.1 2.3 %place.1 = (bf16[128,1024]{1,0:T(8,128)(2,1)}, bf16[128,1024]{1,0:T(8,128)(2,1)}, bf16[128,1024]{1,0:T(8,128)(2,1)}, bf16[128,1024]{1,0:T(8,128)(2,1)}) custom-call(bf16[8,128,128]{2,1,0:T(8,128)(2,1)} %get-tuple-element.6.back, bf16[8,32,128]{2,1,0:T(8,128)(2,1)} %get-tuple-element.7.backx), custom_call_target="tpu_custom_call" | custom-call | tf_op jit(solution)/shard_map/place/pallas_call | solution.py:473

commit v3 on v2

--- a/solution.py
+++ b/solution.py
@@ -51,8 +51,8 @@
 
 
 def exchange_kernel(
-    q_hbm, k_hbm, v_hbm, g_hbm, doc_ref, back, backx,
-    xin, snd, recv, recvx, res, resx, kt, vt, s0, dp0, e_own, dp_own, stat, ot0, dqt0, dkv,
+    q_hbm, k_hbm, v_hbm, g_hbm, doc_hbm, back, backx,
+    doc_ref, xin, snd, recv, recvx, res, resx, kt, vt, s0, dp0, e_own, dp_own, stat, ot0, dqt0, dkv,
     in_sem, send_sem, recv_sem, recvx_sem, ret_sem, back_sem, backx_sem,
 ):
     me = lax.axis_index("seq")
@@ -65,6 +65,8 @@
         pltpu.make_async_copy(ref, xin.at[i], in_sem.at[i])
         for i, ref in enumerate((q_hbm, k_hbm, v_hbm, g_hbm))
     ]
+    load_docs = pltpu.make_async_copy(doc_hbm, doc_ref, in_sem.at[4])
+    load_docs.start()
     for load in loads:
         load.start()
 
@@ -75,16 +77,11 @@
         def _():
             pl.semaphore_signal(barrier, inc=1, device_id={"seq": device}, device_id_type=MESH_ID)
 
-    @pl.when(half == 0)
-    def _():
-        lax.fori_loop(0, H, lambda i, c: (greet(worker_of(i, 0)), c)[1], 0)
-
-    lax.fori_loop(0, H, lambda i, c: (greet(worker_of(i, 1)), c)[1], 0)
-
     @pl.when(is_worker)
     def _():
         lax.fori_loop(0, GROUP * (1 + half), lambda i, c: (greet(i), c)[1], 0)
 
+    load_docs.wait()
     docs = jnp.broadcast_to(doc_ref[...].astype(jnp.float32), (8, TOKENS)).astype(jnp.bfloat16)
     for h in range(H):
         snd[h, 8 * ROWS : MESSAGE] = docs
@@ -96,9 +93,8 @@
             for kind, slot in enumerate(slots):
                 snd[h, slot * ROWS : (slot + 1) * ROWS] = rows[kind * ROWS : (kind + 1) * ROWS]
 
-    own_sources = jnp.where(is_worker, GROUP * (1 + half) - 1, 0)
     own_workers = jnp.where(half == 0, 2 * H, H) - jnp.where(is_worker, 1, 0)
-    pl.semaphore_wait(barrier, own_sources + own_workers)
+    pl.semaphore_wait(barrier, own_workers)
 
 
     def send_main(h):
@@ -113,8 +109,12 @@
             device_id={"seq": worker_of(h, 1)}, device_id_type=MESH_ID,
         )
 
+    def wave_head(i):
+        wave, k = i // 4, lax.rem(i + me, 4)
+        return 2 * k + jnp.where(k < 2, wave, 1 - wave)
+
     def send_head(i, carry):
-        h = lax.rem(i + me, H)
+        h = wave_head(i)
         target = worker_of(h, half)
 
         @pl.when(target != me)
@@ -128,14 +128,15 @@
         return carry
 
     def send_cross_head(i, carry):
-        send_cross(lax.rem(i + me, H)).start()
+        send_cross(wave_head(i)).start()
         return carry
 
-    @pl.when(half == 0)
-    def _():
-        lax.fori_loop(0, H, send_cross_head, 0)
-
-    lax.fori_loop(0, H, send_head, 0)
+    for wave in range(2):
+        @pl.when(half == 0)
+        def _():
+            lax.fori_loop(4 * wave, 4 * wave + 4, send_cross_head, 0)
+
+        lax.fori_loop(4 * wave, 4 * wave + 4, send_head, 0)
 
     @pl.when(is_worker)
     def _():
@@ -408,21 +409,25 @@
         send_back(i)
 
 
-def place_kernel(back, backx, o_ref, dq_ref, dk_ref, dv_ref):
+def place_kernel(back, backx, o_hbm, dq_hbm, dk_hbm, dv_hbm, rows_out, sems):
     first = lax.axis_index("seq") < GROUP
-    for h in range(H):
-        shape = (TOKENS, 2 * ROWS)
-        rank = iota(shape, 1)
-        kind = (h + FINEST * (rank >> 4)) & (CLASSES - 1)
-        spread = (iota(shape, 0) == CLASSES * (rank & (ROWS - 1)) + kind).astype(jnp.bfloat16)
-        lanes = pl.ds(h * HD, HD)
-        for i, ref in enumerate((o_ref, dq_ref, dk_ref, dv_ref)):
+    copies = []
+    for i, ref in enumerate((o_hbm, dq_hbm, dk_hbm, dv_hbm)):
+        for h in range(H):
+            shape = (TOKENS, 2 * ROWS)
+            rank = iota(shape, 1)
+            kind = (h + FINEST * (rank >> 4)) & (CLASSES - 1)
+            spread = (iota(shape, 0) == CLASSES * (rank & (ROWS - 1)) + kind).astype(jnp.bfloat16)
             rows = back[h, 2 * i * ROWS : (2 * i + 2) * ROWS]
             if i >= 2:
-                extra = jnp.where(first, backx[h, (i - 2) * ROWS : (i - 1) * ROWS].astype(jnp.float32), 0.0)
-                summed = (rows[:ROWS].astype(jnp.float32) + extra).astype(jnp.bfloat16)
-                rows = jnp.concatenate([summed, rows[ROWS:]], 0)
-            ref[:, lanes] = dot_nn(spread, rows).astype(jnp.bfloat16)
+                extra = backx[h, (i - 2) * ROWS : (i - 1) * ROWS].astype(jnp.float32)
+                summed = rows[:ROWS].astype(jnp.float32) + jnp.where(first, extra, 0.0)
+                rows = jnp.concatenate([summed.astype(jnp.bfloat16), rows[ROWS:]], 0)
+            rows_out[i, :, h * HD : (h + 1) * HD] = dot_nn(spread, rows).astype(jnp.bfloat16)
+        copies.append(pltpu.make_async_copy(rows_out.at[i], ref, sems.at[i]))
+        copies[-1].start()
+    for copy in copies:
+        copy.wait()
 
 
 def per_device(queries, keys, values, cotangent, doc_ids):
@@ -436,9 +441,10 @@
             jax.ShapeDtypeStruct((H, 8 * ROWS, HD), bf16),
             jax.ShapeDtypeStruct((H, 2 * ROWS, HD), bf16),
         ),
-        in_specs=[any_space] * 4 + [vmem],
+        in_specs=[any_space] * 5,
         out_specs=(any_space, any_space),
         scratch_shapes=[
+            pltpu.VMEM((1, TOKENS), jnp.int32),
             pltpu.VMEM((4, TOKENS, H * HD), bf16),
             pltpu.VMEM((H, MESSAGE, HD), bf16),
             pltpu.VMEM((GROUP, MESSAGE, HD), bf16),
@@ -455,7 +461,7 @@
             pltpu.VMEM((HD, SEG_ROWS), f32),
             pltpu.VMEM((HD, SEG_ROWS), f32),
             pltpu.VMEM((2, 3, SEG_ROWS, HD), f32),
-            dma((4,)),
+            dma((5,)),
             dma,
             dma,
             dma,
@@ -464,17 +470,19 @@
             dma,
         ],
         compiler_params=pltpu.CompilerParams(
-            collective_id=0, has_side_effects=True, vmem_limit_bytes=62 * 2**20
+            collective_id=0, has_side_effects=True, vmem_limit_bytes=28 * 2**20
         ),
         name="exchange",
-    )(queries, keys, values, cotangent, doc_ids.reshape(1, TOKENS))
+    )(*[pltpu.with_memory_space_constraint(a, pltpu.HBM) for a in (queries, keys, values, cotangent, doc_ids.reshape(1, TOKENS))])
     full = jax.ShapeDtypeStruct((TOKENS, H * HD), bf16)
     return tuple(
         pl.pallas_call(
             place_kernel,
             out_shape=(full,) * 4,
             in_specs=[vmem, vmem],
-            out_specs=(vmem,) * 4,
+            out_specs=(any_space,) * 4,
+            scratch_shapes=[pltpu.VMEM((4, TOKENS, H * HD), bf16), dma((4,))],
+            compiler_params=pltpu.CompilerParams(vmem_limit_bytes=16 * 2**20),
             name="place",
         )(back, backx)
     )

time: 38 us -> 35.6 us (0.937); the launches traced: 37.5 us -> 35.5 us
  Pallas kernels: 36.8 us -> 34.8 us
    pallas_call x1, Pallas kernels: 2.35 us -> 1.22 us  [per_device(): pl.pallas_call(place_kernel, out_shape=(full,) * 4, in_specs=[vmem, vmem]...]
    pallas_call x1, Pallas kernels: 34.5 us -> 33.6 us  [per_device(): pl.pallas_call(exchange_kernel, out_shape=(jax.ShapeDtypeStruct((H, 8 * R...]
where the time goes in v3:
time: 35.6 us; the launch traced here: 35.5 us
  Pallas kernels  34.8 us (98%)
  between operations  0.64 us (2%)
    pallas_call x1, Pallas kernels, per_device(): pl.pallas_call(exchange_kernel, out_shape=(jax.ShapeDtypeStruct((H, 8 * R...  33.6 us
    pallas_call x1, Pallas kernels, per_device(): pl.pallas_call(place_kernel, out_shape=(full,) * 4, in_specs=[vmem, vmem]...  1.22 us

profile of v3, /device:TPU:1, one launch (start us, length us, event | category | flops | bytes accessed | tf_op | source)
XLA Modules:
  0.0 35.5 jit_solution(13739480648491261932)
XLA Ops:
  0.6 33.6 %exchange.1 = (bf16[8,128,128]{2,1,0:T(8,128)(2,1)S(1)}, bf16[8,32,128]{2,1,0:T(8,128)(2,1)S(1)}) custom-call(bf16[128,1024]{1,0:T(8,128)(2,1)} %q_hbm.1, bf16[128,1024]{1,0:T(8,128)(2,1)} %k_hbm.1, bf16[128,1024]{1,0:T(8,128)(2,1)} %v_hbm.1, bf16[128,1024]{1,0:T(8,128)(2,1)} %g_hbm.1, s32[1,128]{1,0:T(1,128)} %bitcast.1), custom_call_target="tpu_custom_call" | custom-call | tf_op jit(solution)/shard_map/exchange/pallas_call | solution.py:438
  34.3 1.2 %place.1 = (bf16[128,1024]{1,0:T(8,128)(2,1)}, bf16[128,1024]{1,0:T(8,128)(2,1)}, bf16[128,1024]{1,0:T(8,128)(2,1)}, bf16[128,1024]{1,0:T(8,128)(2,1)}) custom-call(bf16[8,128,128]{2,1,0:T(8,128)(2,1)S(1)} %get-tuple-element.6.back, bf16[8,32,128]{2,1,0:T(8,128)(2,1)S(1)} %get-tuple-element.7.backx), custom_call_target="tpu_custom_call" | custom-call | tf_op jit(solution)/shard_map/place/pallas_call | solution.py:479

commit v4 on v3

--- a/solution.py
+++ b/solution.py
@@ -20,7 +20,7 @@
 MASKED = -1e30
 MESH_ID = pl.DeviceIdType.MESH
 
-MESSAGE = 8 * ROWS + 8
+MESSAGE = 8 * ROWS
 CROSS_AT = 6 * ROWS
 CROSS = MESSAGE - CROSS_AT
 
@@ -52,8 +52,8 @@
 
 def exchange_kernel(
     q_hbm, k_hbm, v_hbm, g_hbm, doc_hbm, back, backx,
-    doc_ref, xin, snd, recv, recvx, res, resx, kt, vt, s0, dp0, e_own, dp_own, stat, ot0, dqt0, dkv,
-    in_sem, send_sem, recv_sem, recvx_sem, ret_sem, back_sem, backx_sem,
+    doc_ref, docs_in, xin, snd, recv, recvx, res, resx, kt, vt, s0, dp0, e_own, dp_own, stat, ot0, dqt0, dkv,
+    in_sem, send_sem, recv_sem, recvx_sem, ret_sem, back_sem, backx_sem, docs_sem,
 ):
     me = lax.axis_index("seq")
     half = me // GROUP
@@ -82,9 +82,6 @@
         lax.fori_loop(0, GROUP * (1 + half), lambda i, c: (greet(i), c)[1], 0)
 
     load_docs.wait()
-    docs = jnp.broadcast_to(doc_ref[...].astype(jnp.float32), (8, TOKENS)).astype(jnp.bfloat16)
-    for h in range(H):
-        snd[h, 8 * ROWS : MESSAGE] = docs
     one_hots = [selector(h).astype(jnp.bfloat16) for h in range(H)]
     for i, slots in enumerate((Q_OF, K_OF, V_OF, D_OF)):
         loads[i].wait()
@@ -103,6 +100,12 @@
             device_id={"seq": worker_of(h, half)}, device_id_type=MESH_ID,
         )
 
+    def send_docs(h, to):
+        return pltpu.make_async_remote_copy(
+            doc_ref, docs_in.at[me], send_sem, docs_sem,
+            device_id={"seq": worker_of(h, to)}, device_id_type=MESH_ID,
+        )
+
     def send_cross(h):
         return pltpu.make_async_remote_copy(
             snd.at[h, pl.ds(CROSS_AT, CROSS)], recvx.at[rank], send_sem, recvx_sem,
@@ -119,15 +122,18 @@
 
         @pl.when(target != me)
         def _():
+            send_docs(h, half).start()
             send_main(h).start()
 
         @pl.when(target == me)
         def _():
+            pltpu.make_async_copy(doc_ref, docs_in.at[me], docs_sem).start()
             pltpu.make_async_copy(snd.at[h], recv.at[rank], recv_sem).start()
 
         return carry
 
     def send_cross_head(i, carry):
+        send_docs(wave_head(i), 1).start()
         send_cross(wave_head(i)).start()
         return carry
 
@@ -142,12 +148,20 @@
     def _():
         pltpu.make_async_copy(recv, recv, recv_sem).wait()
 
+        @pl.when(half == 0)
+        def _():
+            first = docs_in.at[pl.ds(0, GROUP)]
+            pltpu.make_async_copy(first, first, docs_sem).wait()
+
         @pl.when(half == 1)
         def _():
+            pltpu.make_async_copy(docs_in, docs_in, docs_sem).wait()
             pltpu.make_async_copy(recvx, recvx, recvx_sem).wait()
 
         def send_cross_back(i, carry):
-            r = lax.rem(i + rank, GROUP)
+            j = i // 2
+            r = 8 * (j // 8) + lax.rem(j + rank // 2, 8)
+            r = jnp.where(lax.rem(i, 2) == 0, r, GROUP - 1 - r)
             pltpu.make_async_remote_copy(
                 resx.at[r], backx.at[head], ret_sem, backx_sem,
                 device_id={"seq": r}, device_id_type=MESH_ID,
@@ -178,7 +192,7 @@
             lax.fori_loop(0, GROUP, send_cross_back, 0)
 
         attention(
-            head, half, recv, recvx, res, resx, kt, vt, s0, dp0, e_own, dp_own, stat, ot0, dqt0, dkv,
+            head, half, recv, recvx, docs_in, res, resx, kt, vt, s0, dp0, e_own, dp_own, stat, ot0, dqt0, dkv,
             send_crosses, send_back,
         )
 
@@ -191,10 +205,12 @@
     def sent_head(h, carry):
         @pl.when(worker_of(h, half) != me)
         def _():
+            send_docs(h, half).wait_send()
             send_main(h).wait_send()
 
         @pl.when(half == 0)
         def _():
+            send_docs(h, 1).wait_send()
             send_cross(h).wait_send()
 
         return carry
@@ -228,8 +244,8 @@
 
 
 def class_docs(ref, at, kind):
-    eight = ref[:, at : at + 8].astype(jnp.float32)
-    spread = jnp.concatenate([eight, eight], 1).reshape(SEG_ROWS, HD)
+    own_docs = ref[pl.ds(at, GROUP)].astype(jnp.float32)
+    spread = jnp.broadcast_to(own_docs, (GROUP, ROWS, HD)).reshape(SEG_ROWS, HD)
     shape = (SEG_ROWS, HD)
     own = iota(shape, 1) == CLASSES * (iota(shape, 0) & (ROWS - 1)) + kind
     picked = jnp.where(own, spread, 0.0).astype(jnp.bfloat16)
@@ -238,7 +254,7 @@
 
 
 def attention(
-    head, half, recv, recvx, res, resx, kt, vt, s0, dp0, e_own, dp_own, stat, ot0, dqt0, dkv,
+    head, half, recv, recvx, docs_in, res, resx, kt, vt, s0, dp0, e_own, dp_own, stat, ot0, dqt0, dkv,
     send_crosses, send_back,
 ):
     bf16, f32 = jnp.bfloat16, jnp.float32
@@ -252,7 +268,7 @@
     for kind in (0, 1):
         kt[kind] = dot_nt(eye, k_all[kind]).astype(bf16)
         vt[kind] = dot_nt(eye, v_all[kind]).astype(bf16)
-    docs = [class_docs(recv, 8 * ROWS, (head + FINEST * kind) & (CLASSES - 1)) for kind in (0, 1)]
+    docs = [class_docs(docs_in, GROUP * half, (head + FINEST * kind) & (CLASSES - 1)) for kind in (0, 1)]
     cols = [d[0] for d in docs]
     q_docs = [d[1][0:1] for d in docs]
 
@@ -264,7 +280,7 @@
 
     @pl.when(half == 1)
     def _():
-        col0, _ = class_docs(recvx, 2 * ROWS, head)
+        col0, _ = class_docs(docs_in, 0, head)
         k0 = tile_rows(recvx, 0)
         kt[2] = dot_nt(eye, k0).astype(bf16)
         vt[2] = dot_nt(eye, tile_rows(recvx, 1)).astype(bf16)
@@ -445,6 +461,7 @@
         out_specs=(any_space, any_space),
         scratch_shapes=[
             pltpu.VMEM((1, TOKENS), jnp.int32),
+            pltpu.VMEM((SEQ_DEVICES, 1, TOKENS), jnp.int32),
             pltpu.VMEM((4, TOKENS, H * HD), bf16),
             pltpu.VMEM((H, MESSAGE, HD), bf16),
             pltpu.VMEM((GROUP, MESSAGE, HD), bf16),
@@ -462,6 +479,7 @@
             pltpu.VMEM((HD, SEG_ROWS), f32),
             pltpu.VMEM((2, 3, SEG_ROWS, HD), f32),
             dma((5,)),
+            dma,
             dma,
             dma,
             dma,

time: 35.6 us -> 35.3 us (level)
  no operation moved by 1% of the time
where the time goes in v4:
time: 35.3 us; the launch traced here: 35.2 us
  Pallas kernels  34.5 us (98%)
  between operations  0.64 us (2%)
    pallas_call x1, Pallas kernels, per_device(): pl.pallas_call(exchange_kernel, out_shape=(jax.ShapeDtypeStruct((H, 8 * R...  33.3 us
    pallas_call x1, Pallas kernels, per_device(): pl.pallas_call(place_kernel, out_shape=(full,) * 4, in_specs=[vmem, vmem]...  1.22 us

profile of v4, /device:TPU:1, one launch (start us, length us, event | category | flops | bytes accessed | tf_op | source)
XLA Modules:
  0.0 35.2 jit_solution(9437059928219270781)
XLA Ops:
  0.6 33.3 %exchange.1 = (bf16[8,128,128]{2,1,0:T(8,128)(2,1)S(1)}, bf16[8,32,128]{2,1,0:T(8,128)(2,1)S(1)}) custom-call(bf16[128,1024]{1,0:T(8,128)(2,1)} %q_hbm.1, bf16[128,1024]{1,0:T(8,128)(2,1)} %k_hbm.1, bf16[128,1024]{1,0:T(8,128)(2,1)} %v_hbm.1, bf16[128,1024]{1,0:T(8,128)(2,1)} %g_hbm.1, s32[1,128]{1,0:T(1,128)} %bitcast.1), custom_call_target="tpu_custom_call" | custom-call | tf_op jit(solution)/shard_map/exchange/pallas_call | solution.py:454
  34.0 1.2 %place.1 = (bf16[128,1024]{1,0:T(8,128)(2,1)}, bf16[128,1024]{1,0:T(8,128)(2,1)}, bf16[128,1024]{1,0:T(8,128)(2,1)}, bf16[128,1024]{1,0:T(8,128)(2,1)}) custom-call(bf16[8,128,128]{2,1,0:T(8,128)(2,1)S(1)} %get-tuple-element.6.back, bf16[8,32,128]{2,1,0:T(8,128)(2,1)S(1)} %get-tuple-element.7.backx), custom_call_target="tpu_custom_call" | custom-call | tf_op jit(solution)/shard_map/place/pallas_call | solution.py:497

commit v5 on v4

--- a/solution.py
+++ b/solution.py
@@ -168,7 +168,9 @@
             ).start()
             return carry
 
-        def send_back(block):
+        def send_back(block, start, size):
+            part = pl.ds(start, size)
+
             def one(i, carry):
                 r = block * 8 + lax.rem(i + rank, 8)
                 target = GROUP * half + r
@@ -176,13 +178,13 @@
                 @pl.when(target != me)
                 def _():
                     pltpu.make_async_remote_copy(
-                        res.at[r], back.at[head], ret_sem, back_sem,
+                        res.at[r, part], back.at[head, part], ret_sem, back_sem,
                         device_id={"seq": target}, device_id_type=MESH_ID,
                     ).start()
 
                 @pl.when(target == me)
                 def _():
-                    pltpu.make_async_copy(res.at[r], back.at[head], back_sem).start()
+                    pltpu.make_async_copy(res.at[r, part], back.at[head, part], back_sem).start()
 
                 return carry
 
@@ -386,8 +388,7 @@
         resx[:, ROWS:] = dkv[1, 2].astype(bf16).reshape(GROUP, ROWS, HD)
         send_crosses()
 
-    started = False
-    for i in reversed(range(blocks)):
+    for i in (0, 3, 2, 1):
         at = pl.ds(i * HD, HD)
         n = (i + 1) * HD
         total = jnp.concatenate([stat[1, 0:1, at], totals[i][:, HD:]], 1)
@@ -403,26 +404,36 @@
             out_t = out_t + dot_nn(vt[kind, :, :n], w)
             dq_t = dq_t + dot_nn(kt[kind, :, :n], ds)
             dk, dv = dot_nn(ds, qs[i]), dot_nn(w, gs[i])
-            if started:
-                dk = dk + dkv[0, kind, :n]
-                dv = dv + dkv[1, kind, :n]
-            dkv[0, kind, :n] = dk
-            dkv[1, kind, :n] = dv
-        started = True
+            done = {0: 0, 3: HD, 2: n, 1: n}[i]
+            for which, part in enumerate((dk, dv)):
+                if done:
+                    dkv[which, kind, :done] += part[:done]
+                if done < n:
+                    dkv[which, kind, done:n] = part[done:]
         out = dot_nt(eye_block, out_t.astype(bf16)).astype(bf16)
         dq = dot_nt(eye_block, (dq_t * SCORE_SCALE).astype(bf16)).astype(bf16)
         owners = slice(8 * i, 8 * i + 8)
         for kind in (0, 1):
-            tiles = (
-                out[kind * HD : (kind + 1) * HD],
-                dq[kind * HD : (kind + 1) * HD],
-                (dkv[0, kind, at] * SCORE_SCALE).astype(bf16),
-                dkv[1, kind, at].astype(bf16),
-            )
-            for t, tile in enumerate(tiles):
+            rows = slice(kind * HD, (kind + 1) * HD)
+            for t, tile in enumerate((out[rows], dq[rows])):
                 slot = (2 * t + kind) * ROWS
                 res[owners, slot : slot + ROWS] = tile.reshape(8, ROWS, HD)
-        send_back(i)
+        if i:
+            store_keys(dkv, res, i)
+            send_back(i, 0, 8 * ROWS)
+        else:
+            send_back(i, 0, 4 * ROWS)
+    store_keys(dkv, res, 0)
+    send_back(0, 4 * ROWS, 4 * ROWS)
+
+
+def store_keys(dkv, res, block):
+    at = pl.ds(block * HD, HD)
+    owners = slice(8 * block, 8 * block + 8)
+    for kind in (0, 1):
+        for t, tile in enumerate((dkv[0, kind, at] * SCORE_SCALE, dkv[1, kind, at])):
+            slot = (4 + 2 * t + kind) * ROWS
+            res[owners, slot : slot + ROWS] = tile.astype(jnp.bfloat16).reshape(8, ROWS, HD)
 
 
 def place_kernel(back, backx, o_hbm, dq_hbm, dk_hbm, dv_hbm, rows_out, sems):

time: 35.3 us -> 35.2 us (level)
  no operation moved by 1% of the time
where the time goes in v5:
time: 35.2 us; the launch traced here: 35 us
  Pallas kernels  34.3 us (97%)
  between operations  0.64 us (2%)
    pallas_call x1, Pallas kernels, per_device(): pl.pallas_call(exchange_kernel, out_shape=(jax.ShapeDtypeStruct((H, 8 * R...  33.1 us
    pallas_call x1, Pallas kernels, per_device(): pl.pallas_call(place_kernel, out_shape=(full,) * 4, in_specs=[vmem, vmem]...  1.22 us

profile of v5, /device:TPU:1, one launch (start us, length us, event | category | flops | bytes accessed | tf_op | source)
XLA Modules:
  0.0 35.0 jit_solution(10449338797078615436)
XLA Ops:
  0.6 33.1 %exchange.1 = (bf16[8,128,128]{2,1,0:T(8,128)(2,1)S(1)}, bf16[8,32,128]{2,1,0:T(8,128)(2,1)S(1)}) custom-call(bf16[128,1024]{1,0:T(8,128)(2,1)} %q_hbm.1, bf16[128,1024]{1,0:T(8,128)(2,1)} %k_hbm.1, bf16[128,1024]{1,0:T(8,128)(2,1)} %v_hbm.1, bf16[128,1024]{1,0:T(8,128)(2,1)} %g_hbm.1, s32[1,128]{1,0:T(1,128)} %bitcast.1), custom_call_target="tpu_custom_call" | custom-call | tf_op jit(solution)/shard_map/exchange/pallas_call | solution.py:465
  33.8 1.2 %place.1 = (bf16[128,1024]{1,0:T(8,128)(2,1)}, bf16[128,1024]{1,0:T(8,128)(2,1)}, bf16[128,1024]{1,0:T(8,128)(2,1)}, bf16[128,1024]{1,0:T(8,128)(2,1)}) custom-call(bf16[8,128,128]{2,1,0:T(8,128)(2,1)S(1)} %get-tuple-element.6.back, bf16[8,32,128]{2,1,0:T(8,128)(2,1)S(1)} %get-tuple-element.7.backx), custom_call_target="tpu_custom_call" | custom-call | tf_op jit(solution)/shard_map/place/pallas_call | solution.py:508
